TPU v7x, 32 devices: a whole 2x2x4 slice. The times are simulated.
32 devices in a mesh: member: 4 (over y, x), slab: 2 (over core), tile: 4 (over z).
Axes of the slice: x: 2, y: 2, z: 4, core: 2. Of those that a mesh axis runs over, the one named last changes fastest.
Arguments:
- prior: float32 [128, 32768], P('member', ('slab', 'tile')), may hold values from -6 to 6
- sensitivity: bfloat16 [64, 16, 64, 512], P(('slab', 'tile')), may hold values from -0.0625 to 0.0625
- pattern: int32 [64, 16], P(('slab', 'tile')), may hold values from -1 to 63, as said below
- ownership: int32 [64], replicated, may hold values from 0 to 63, each once
- observed: float32 [4096], P(('slab', 'tile')), may hold values from -8 to 8
- obs_noise: float32 [4096], P(('slab', 'tile')), may hold values from 0.3 to 3
- perturbation: float32 [128, 4096], P('member', ('slab', 'tile')), may hold values from -5 to 5
Outputs:
- increment: float32 [128, 32768], P('member', ('slab', 'tile'))
- weights: float32 [128, 128], replicated
Inputs may be any that keep to these rules, and one draw needn't show every extreme that they name: In each row of pattern the first c entries are distinct observation block numbers and the remaining 16 - c entries are -1, with 4 <= c <= 16; some row is full and some row has exactly 4 live entries.
All inputs are finite; a program needn't handle non-finite values.
Results may differ from a plain program's by a relative error of at most 0.0042.
Values may be sent and summed in bfloat16 or wider, within the bound.
No kernel may reach another device: no remote copies, remote signals or barrier semaphores. Data moves between devices by JAX's collectives and lax.ppermute only.
A program may use at most 64 MiB of HBM per device.

v0:
```python
import functools
import math

import jax
import jax.numpy as jnp
from jax import lax
from jax.experimental import pallas as pl
from jax.experimental.pallas import tpu as pltpu
from jax.sharding import PartitionSpec as P


EXACT = lax.Precision.HIGHEST
VMEM = pl.BlockSpec(memory_space=pltpu.VMEM)
SMEM = pl.BlockSpec(memory_space=pltpu.SMEM)
NT = (((1,), (1,)), ((), ()))


def swap(x, axis, distance):
    size = lax.axis_size(axis)
    return lax.ppermute(x, axis, [(i, i ^ distance) for i in range(size)])


def digits(size):
    out, shift = [], 0
    while size > 1:
        radix = 4 if size % 4 == 0 else 2
        out.append((shift, radix))
        shift += radix.bit_length() - 1
        size //= radix
    return out[::-1]


def gather_xor(x, axis):
    return [x] + [swap(x, axis, r) for r in range(1, lax.axis_size(axis))]


def contribute_kernel(
    owned,
    depth,
    pattern_ref,
    ownership_ref,
    prior_hbm,
    sens_hbm,
    keep_ref,
    send_ref,
    bf_ref,
    sens,
    prior,
    acc,
    storage,
    sens_sems,
    prior_sems,
):
    blocks, slots = pattern_ref.shape
    tiles, _, lanes = keep_ref.shape
    members_dev = prior.shape[0]
    _, rows_block, params = sens.shape
    obs_block = rows_block // slots
    copies = lanes // members_dev
    groups = owned // copies
    me = lax.axis_index("slab") * tiles + lax.axis_index("tile")

    def cols(b):
        return pl.ds(pl.multiple_of(b * params, params), params)

    def fetch(b):
        return (
            pltpu.make_async_copy(prior_hbm.at[:, cols(b)], prior.at[:, cols(b)], prior_sems.at[b]),
            pltpu.make_async_copy(sens_hbm.at[b], sens.at[b], sens_sems.at[b]),
        )

    for b in range(depth):
        for copy in fetch(b):
            copy.start()

    def place(s, carry):
        storage[ownership_ref[s]] = s ^ (me * owned)
        return carry

    lax.fori_loop(0, ownership_ref.shape[0], place, 0, unroll=8)
    acc[...] = jnp.zeros_like(acc)
    lane_group = lax.broadcasted_iota(jnp.int32, (obs_block, lanes), 1) // members_dev

    def work(b, carry):
        @pl.when(b + depth < blocks)
        def _():
            for copy in fetch(b + depth):
                copy.start()

        for copy in fetch(b):
            copy.wait()
        rows = prior[:, cols(b)].astype(jnp.bfloat16)
        bf_ref[:, cols(b)] = rows
        terms = lax.dot_general(
            sens[b],
            jnp.concatenate([rows] * copies, axis=0),
            NT,
            preferred_element_type=jnp.float32,
        )
        for k in range(slots):
            block = pattern_ref[b, k]
            at = storage[jnp.maximum(block, 0)]
            group = jnp.where(block >= 0, (at % owned) // groups, -1)
            acc[(at // owned) * groups + at % groups] += jnp.where(
                lane_group == group, terms[k * obs_block : (k + 1) * obs_block], 0.0
            )
        return carry

    lax.fori_loop(0, blocks, work, 0)

    def flush(r, carry):
        for g in range(groups):
            rows = slice(g * obs_block, (g + 1) * obs_block)
            keep_ref[r, rows, :] = acc[r * groups + g]
            send_ref[r, rows, :] = acc[(tiles + r) * groups + g]
        return carry

    lax.fori_loop(0, tiles, flush, 0, unroll=4)


def contribute(prior, sensitivity, pattern, ownership, obs_dev):
    members_dev = prior.shape[0]
    blocks, slots, obs_block, params = sensitivity.shape
    tiles = lax.axis_size("tile")
    owned = obs_dev // obs_block
    lanes = 128
    groups = owned // (lanes // members_dev)
    half = jax.ShapeDtypeStruct((tiles, groups * obs_block, lanes), jnp.float32)
    hbm = pl.BlockSpec(memory_space=pl.ANY)
    return pl.pallas_call(
        functools.partial(contribute_kernel, owned, min(3, blocks)),
        in_specs=[SMEM, SMEM, hbm, hbm],
        out_specs=[VMEM, VMEM, VMEM],
        out_shape=[half, half, jax.ShapeDtypeStruct(prior.shape, jnp.bfloat16)],
        scratch_shapes=[
            pltpu.VMEM((blocks, slots * obs_block, params), jnp.bfloat16),
            pltpu.VMEM(prior.shape, jnp.float32),
            pltpu.VMEM((2 * tiles * groups, obs_block, lanes), jnp.float32),
            pltpu.SMEM(ownership.shape, jnp.int32),
            pltpu.SemaphoreType.DMA((blocks,)),
            pltpu.SemaphoreType.DMA((blocks,)),
        ],
        name="contribute",
    )(pattern, ownership, prior, sensitivity.reshape(blocks, slots * obs_block, params))


def gram_kernel(count, *refs):
    predicted, noise = refs[:count], refs[count : 2 * count]
    observed, sigma, keep, send, stack, whole = refs[2 * count :]
    members_dev = noise[0].shape[0]
    members = members_dev * count
    width, lanes = predicted[0].shape
    at = lax.axis_index("member")
    for r in range(count):
        rows = pl.ds(pl.multiple_of((at ^ r) * members_dev, members_dev), members_dev)
        turned = predicted[r][...].T
        for q in range(lanes // members_dev):
            stack[rows, q * width : (q + 1) * width] = turned[
                q * members_dev : (q + 1) * members_dev
            ]
        whole_rows = pl.ds(pl.multiple_of(members + (at ^ r) * members_dev, members_dev), members_dev)
        stack[whole_rows, :] = noise[r][...]
    values = stack[:members, :]
    inverse = 1.0 / sigma[...]
    spread = (values - jnp.mean(values, axis=0, keepdims=True)) * (
        inverse * (1.0 / math.sqrt(members - 1))
    )
    innovation = (observed[...] - values) * inverse + stack[members:, :]
    stack[:members, :] = spread
    stack[members:, :] = innovation
    misfit = jnp.sum(jnp.sum(innovation * innovation, axis=0, keepdims=True), axis=1, keepdims=True)
    both = lax.dot_general(
        spread, stack[...], NT, precision=EXACT, preferred_element_type=jnp.float32
    )
    row = lax.broadcasted_iota(jnp.int32, both.shape, 0)
    col = lax.broadcasted_iota(jnp.int32, both.shape, 1)
    whole[...] = both + jnp.where(row == col, misfit * (1.0 / (4.0 * members * members)), 0.0)
    rows = members // 2
    side = lax.axis_index("slab")
    keep[...] = whole[pl.ds(pl.multiple_of(side * rows, rows), rows), :]
    send[...] = whole[pl.ds(pl.multiple_of((1 - side) * rows, rows), rows), :]


def gram(predicted, noise, observed, sigma):
    count = len(predicted)
    members_dev, obs_dev = noise[0].shape
    members = members_dev * count
    half = jax.ShapeDtypeStruct((members // 2, 2 * members), jnp.float32)
    return pl.pallas_call(
        functools.partial(gram_kernel, count),
        in_specs=[VMEM] * (2 * count + 2),
        out_specs=[VMEM, VMEM],
        out_shape=[half, half],
        scratch_shapes=[
            pltpu.VMEM((2 * members, obs_dev), jnp.float32),
            pltpu.VMEM((members, 2 * members), jnp.float32),
        ],
        compiler_params=pltpu.CompilerParams(vmem_limit_bytes=8 << 20),
        name="gram",
    )(*predicted, *noise, observed.reshape(1, obs_dev), sigma.reshape(1, obs_dev))


def update_kernel(count, *refs):
    mine, other = refs[:2]
    prior = refs[2 : 2 + count]
    increment, weights, both, cols, ensemble, sems = refs[2 + count :]
    members = weights.shape[0]
    members_dev = members // count
    at = lax.axis_index("member")
    side = lax.axis_index("slab")
    copies = []
    for r in range(count):
        rows = pl.ds(pl.multiple_of((at ^ r) * members_dev, members_dev), members_dev)
        copies.append(pltpu.make_async_copy(prior[r], ensemble.at[rows, :], sems.at[r]))
        copies[-1].start()
    half = members // 2
    both[pl.ds(pl.multiple_of(side * half, half), half), :] = mine[...]
    both[pl.ds(pl.multiple_of((1 - side) * half, half), half), :] = other[...]
    row = lax.broadcasted_iota(jnp.int32, (members, members), 0)
    col = lax.broadcasted_iota(jnp.int32, (members, members), 1)
    eye = jnp.where(row == col, 1.0, 0.0)
    system = both[:, :members]

    def total(x):
        return jnp.sum(jnp.sum(x, axis=0, keepdims=True), axis=1, keepdims=True)

    trace = total(system * eye)
    system = system + trace * (1.0 / (members * members))
    bound = jnp.max(jnp.sum(jnp.abs(system), axis=0, keepdims=True), axis=1, keepdims=True)
    scale = jnp.minimum(trace * (1.0 + 1.0 / members) / total(system * system), 1.9 / bound)
    power = eye - scale * system
    terms = both[:, members:] * scale

    def step(power, terms):
        pair = lax.dot_general(
            power,
            jnp.concatenate([power, terms], axis=1),
            (((1,), (0,)), ((), ())),
            precision=EXACT,
            preferred_element_type=jnp.float32,
        )
        return pair[:, :members], terms + pair[:, members:]

    for _ in range(5):
        power, terms = step(power, terms)

    def unfinished(carry):
        power, _, count = carry
        return (jnp.sum(power * power) > 1e-12) & (count < 40)

    def further(carry):
        power, terms, count = carry
        power, terms = step(power, terms)
        return power, terms, count + 1

    _, terms, _ = lax.while_loop(unfinished, further, (power, terms, 0))
    weights[...] = terms
    centred = (terms - jnp.mean(terms, axis=0, keepdims=True)) * (1.0 / math.sqrt(members - 1))
    cols[...] = centred.T
    own = cols[pl.ds(pl.multiple_of(at * members_dev, members_dev), members_dev), :].astype(
        jnp.bfloat16
    )
    for copy in copies:
        copy.wait()
    width = 512

    def multiply(n, carry):
        lanes = pl.ds(pl.multiple_of(n * width, width), width)
        increment[:, lanes] = jnp.dot(own, ensemble[:, lanes], preferred_element_type=jnp.float32)
        return carry

    lax.fori_loop(0, increment.shape[1] // width, multiply, 0, unroll=True)


def update(mine, other, prior):
    count = len(prior)
    members_dev, params = prior[0].shape
    members = members_dev * count
    return pl.pallas_call(
        functools.partial(update_kernel, count),
        in_specs=[VMEM, VMEM] + [pl.BlockSpec(memory_space=pl.ANY)] * count,
        out_specs=[VMEM, VMEM],
        out_shape=[
            jax.ShapeDtypeStruct((members_dev, params), jnp.float32),
            jax.ShapeDtypeStruct((members, members), jnp.float32),
        ],
        scratch_shapes=[
            pltpu.VMEM((members, 2 * members), jnp.float32),
            pltpu.VMEM((members, members), jnp.float32),
            pltpu.VMEM((members, params), jnp.bfloat16),
            pltpu.SemaphoreType.DMA((count,)),
        ],
        compiler_params=pltpu.CompilerParams(vmem_limit_bytes=8 << 20),
        name="update",
    )(mine, other, *prior)


def step(prior, sensitivity, pattern, ownership, observed, obs_noise, perturbation):
    obs_dev = observed.shape[0]
    tiles = lax.axis_size("tile")
    keep, send, prior_bf = contribute(prior, sensitivity, pattern, ownership, obs_dev)
    got = swap(send, "slab", 1)
    chunks = [keep[r] + got[r] for r in range(tiles)]
    chunks, perturbation = lax.optimization_barrier((chunks, perturbation))
    noise = gather_xor(perturbation, "member")
    ensemble = gather_xor(prior_bf, "member")
    for shift, radix in digits(tiles):
        low = 1 << shift
        arrived = [
            [swap(chunks[d * low + r], "tile", d << shift) for r in range(low)]
            for d in range(1, radix)
        ]
        chunks = [sum((g[r] for g in arrived), chunks[r]) for r in range(low)]
    predicted = gather_xor(chunks[0], "member")
    keep, send = gram(predicted, noise, observed, obs_noise)
    mine = keep + swap(send, "slab", 1)
    for shift, radix in digits(tiles)[::-1]:
        mine = sum((swap(mine, "tile", d << shift) for d in range(1, radix)), mine)
    return tuple(update(mine, swap(mine, "slab", 1), ensemble))


def solution(mesh):
    return jax.shard_map(
        step,
        mesh=mesh,
        in_specs=(
            P("member", ("slab", "tile")),
            P(("slab", "tile"), None, None, None),
            P(("slab", "tile"), None),
            P(),
            P(("slab", "tile")),
            P(("slab", "tile")),
            P("member", ("slab", "tile")),
        ),
        out_specs=(P("member", ("slab", "tile")), P()),
        check_vma=False,
    )
```

profile of v0, /device:TPU:0, one launch (start us, length us, event | category | flops | bytes accessed | tf_op | source)
XLA Modules:
  0.0 55.4 jit_solution(7935050164182900941)
XLA Ops:
  0.7 6.8 %contribute.1 = (f32[4,128,128]{2,1,0:T(8,128)}, f32[4,128,128]{2,1,0:T(8,128)}, bf16[32,4096]{1,0:T(8,128)(2,1)}) custom-call(s32[8,16]{1,0:T(8,128)} %pattern_ref.1, s32[64]{0:T(128)} %ownership_ref.1, f32[32,4096]{1,0:T(8,128)} %prior_hbm.1, bf16[8,1024,512]{2,1,0:T(8,128)(2,1)} %bitcast.13), custom_call_target="tpu_custom_call" | custom-call | tf_op jit(solution)/shard_map/contribute/pallas_call | solution.py:130
  7.4 0.6 %collective-permute-start = (f32[4,128,128]{2,1,0:T(8,128)}, f32[4,128,128]{2,1,0:T(8,128)S(1)}, u32[]{:S(2)}, u32[]{:S(2)}) collective-permute-start(f32[4,128,128]{2,1,0:T(8,128)} %get-tuple-element.13), channel_id=1, source_target_pairs={{0,4},{4,0},{1,5},{5,1},{2,6},{6,2},{3,7},{7,3},{8,12},{12,8},{9,1... | collective-permute-start | bytes 786440 | tf_op jit(solution)/shard_map/ppermute | solution.py:20
  8.0 1.4 %collective-permute-done = f32[4,128,128]{2,1,0:T(8,128)S(1)} collective-permute-done((f32[4,128,128]{2,1,0:T(8,128)}, f32[4,128,128]{2,1,0:T(8,128)S(1)}, u32[]{:S(2)}, u32[]{:S(2)}) %collective-permute-start) | collective-permute-done | bytes 262176 | tf_op jit(solution)/shard_map/ppermute | solution.py:20
  9.4 1.0 %fusion = (f32[128,128]{1,0:T(8,128)S(1)}, f32[128,128]{1,0:T(8,128)S(1)}, f32[128,128]{1,0:T(8,128)S(1)}, f32[128,128]{1,0:T(8,128)S(1)}) fusion(f32[4,128,128]{2,1,0:T(8,128)S(1)} %collective-permute-done, f32[4,128,128]{2,1,0:T(8,128)} %get-tuple-element.12), kind=kLoop, calls=%fused_computation.1 | loop fusion | flops 65536 | bytes 786432 | tf_op jit(solution)/shard_map/add | solution.py:303
  10.4 3.0 %collective-permute-start.1 = (f32[128,128]{1,0:T(8,128)S(1)}, f32[128,128]{1,0:T(8,128)S(1)}, u32[]{:S(2)}, u32[]{:S(2)}) collective-permute-start(f32[128,128]{1,0:T(8,128)S(1)} %get-tuple-element.15), channel_id=1, source_target_pairs={{0,1},{1,0},{2,3},{3,2},{4,5},{5,4},{6,7},{7,6},{8,9},{9,8},{10,11... | collective-permute-start | bytes 196616 | tf_op jit(solution)/shard_map/ppermute | solution.py:20
  13.3 2.6 %collective-permute-start.2 = (f32[128,128]{1,0:T(8,128)S(1)}, f32[128,128]{1,0:T(8,128)S(1)}, u32[]{:S(2)}, u32[]{:S(2)}) collective-permute-start(f32[128,128]{1,0:T(8,128)S(1)} %get-tuple-element.16), channel_id=1, source_target_pairs={{0,2},{1,3},{2,0},{3,1},{4,6},{5,7},{6,4},{7,5},{8,10},{9,11},{10,... | collective-permute-start | bytes 196616 | tf_op jit(solution)/shard_map/ppermute | solution.py:20
  15.9 2.7 %collective-permute-start.9 = (f32[32,512]{1,0:T(8,128)S(1)}, f32[32,512]{1,0:T(8,128)S(1)}, u32[]{:S(2)}, u32[]{:S(2)}) collective-permute-start(f32[32,512]{1,0:T(8,128)S(1)} %copy-done.1), channel_id=1, source_target_pairs={{0,24},{8,16},{16,8},{24,0},{1,25},{9,17},{17,9},{25,1},{2,26},{10... | collective-permute-start | bytes 196616 | tf_op jit(solution)/shard_map/ppermute | solution.py:20
  19.4 1.4 %collective-permute-done.2 = f32[128,128]{1,0:T(8,128)S(1)} collective-permute-done((f32[128,128]{1,0:T(8,128)S(1)}, f32[128,128]{1,0:T(8,128)S(1)}, u32[]{:S(2)}, u32[]{:S(2)}) %collective-permute-start.2) | collective-permute-done | bytes 65568 | tf_op jit(solution)/shard_map/ppermute | solution.py:20
  20.9 1.2 %collective-permute-done.3 = f32[128,128]{1,0:T(8,128)S(1)} collective-permute-done((f32[128,128]{1,0:T(8,128)S(1)}, f32[128,128]{1,0:T(8,128)S(1)}, u32[]{:S(2)}, u32[]{:S(2)}) %collective-permute-start.3) | collective-permute-done | bytes 65568 | tf_op jit(solution)/shard_map/ppermute | solution.py:20
  22.1 2.5 %collective-permute-start.6 = (f32[128,128]{1,0:T(8,128)S(1)}, f32[128,128]{1,0:T(8,128)S(1)}, u32[]{:S(2)}, u32[]{:S(2)}) collective-permute-start(f32[128,128]{1,0:T(8,128)S(1)} %add_add_fusion.1.refs_0_), channel_id=1, source_target_pairs={{0,24},{8,16},{16,8},{24,0},{1,25},{9,17},{17,9},{25,1},{2,26},{10... | collective-permute-start | bytes 196616 | tf_op jit(solution)/shard_map/ppermute | solution.py:20
  25.2 0.5 collective-permute-start.4
  25.7 2.3 %collective-permute-done.6.refs_3_ = f32[128,128]{1,0:T(8,128)S(1)} collective-permute-done((f32[128,128]{1,0:T(8,128)S(1)}, f32[128,128]{1,0:T(8,128)S(1)}, u32[]{:S(2)}, u32[]{:S(2)}) %collective-permute-start.6) | collective-permute-done | bytes 65568 | tf_op jit(solution)/shard_map/ppermute | solution.py:20
  28.0 0.9 %collective-permute-done.5.refs_2_ = f32[128,128]{1,0:T(8,128)S(1)} collective-permute-done((f32[128,128]{1,0:T(8,128)S(1)}, f32[128,128]{1,0:T(8,128)S(1)}, u32[]{:S(2)}, u32[]{:S(2)}) %collective-permute-start.5) | collective-permute-done | bytes 65568 | tf_op jit(solution)/shard_map/ppermute | solution.py:20
  29.4 0.9 %gram.1 = (f32[64,256]{1,0:T(8,128)S(1)}, f32[64,256]{1,0:T(8,128)S(1)}) custom-call(f32[128,128]{1,0:T(8,128)S(1)} %add_add_fusion.1.refs_0_, f32[128,128]{1,0:T(8,128)S(1)} %collective-permute-done.4.refs_1_, f32[128,128]{1,0:T(8,128)S(1)} %collective-permute-done.5.refs_2_, f32[128,128]{1,0:T(8,128)S(1)} %collective-permute-done.6.refs_3_, ...), custom_call_target="tpu_custom_call" | custom-call | tf_op jit(solution)/shard_map/gram/pallas_call | solution.py:189
  30.4 1.2 %collective-permute-done.10 = f32[64,256]{1,0:T(8,128)S(1)} collective-permute-done((f32[64,256]{1,0:T(8,128)S(1)}, f32[64,256]{1,0:T(8,128)S(1)}, u32[]{:S(2)}, u32[]{:S(2)}) %collective-permute-start.10) | collective-permute-done | bytes 65568 | tf_op jit(solution)/shard_map/ppermute | solution.py:20
  31.7 2.1 %collective-permute-start.13 = (f32[64,256]{1,0:T(8,128)S(1)}, f32[64,256]{1,0:T(8,128)S(1)}, u32[]{:S(2)}, u32[]{:S(2)}) collective-permute-start(f32[64,256]{1,0:T(8,128)S(1)} %add.56), channel_id=1, source_target_pairs={{0,3},{1,2},{2,1},{3,0},{4,7},{5,6},{6,5},{7,4},{8,11},{9,10},{10,... | collective-permute-start | bytes 196616 | tf_op jit(solution)/shard_map/ppermute | solution.py:20
  34.0 2.1 %collective-permute-start.11 = (f32[64,256]{1,0:T(8,128)S(1)}, f32[64,256]{1,0:T(8,128)S(1)}, u32[]{:S(2)}, u32[]{:S(2)}) collective-permute-start(f32[64,256]{1,0:T(8,128)S(1)} %add.56), channel_id=1, source_target_pairs={{0,1},{1,0},{2,3},{3,2},{4,5},{5,4},{6,7},{7,6},{8,9},{9,8},{10,11... | collective-permute-start | bytes 196616 | tf_op jit(solution)/shard_map/ppermute | solution.py:20
  36.1 1.5 %collective-permute-start.17 = (bf16[32,4096]{1,0:T(8,128)(2,1)}, bf16[32,4096]{1,0:T(8,128)(2,1)S(1)}, u32[]{:S(2)}, u32[]{:S(2)}) collective-permute-start(bf16[32,4096]{1,0:T(8,128)(2,1)} %get-tuple-element.21.refs_2_), channel_id=1, source_target_pairs={{0,24},{8,16},{16,8},{24,0},{1,25},{9,17},{17,9},{25,1},{2,26},{10... | collective-permute-start | bytes 786440 | tf_op jit(solution)/shard_map/ppermute | solution.py:20
  38.5 1.1 %collective-permute-start.15 = (bf16[32,4096]{1,0:T(8,128)(2,1)}, bf16[32,4096]{1,0:T(8,128)(2,1)S(1)}, u32[]{:S(2)}, u32[]{:S(2)}) collective-permute-start(bf16[32,4096]{1,0:T(8,128)(2,1)} %get-tuple-element.21.refs_2_), channel_id=1, source_target_pairs={{0,8},{8,0},{16,24},{24,16},{1,9},{9,1},{17,25},{25,17},{2,10},{10... | collective-permute-start | bytes 786440 | tf_op jit(solution)/shard_map/ppermute | solution.py:20
  39.6 0.9 %collective-permute-done.12 = f32[64,256]{1,0:T(8,128)S(1)} collective-permute-done((f32[64,256]{1,0:T(8,128)S(1)}, f32[64,256]{1,0:T(8,128)S(1)}, u32[]{:S(2)}, u32[]{:S(2)}) %collective-permute-start.12) | collective-permute-done | bytes 65568 | tf_op jit(solution)/shard_map/ppermute | solution.py:20
  40.6 5.9 %collective-permute-done.17.refs_5_ = bf16[32,4096]{1,0:T(8,128)(2,1)S(1)} collective-permute-done((bf16[32,4096]{1,0:T(8,128)(2,1)}, bf16[32,4096]{1,0:T(8,128)(2,1)S(1)}, u32[]{:S(2)}, u32[]{:S(2)}) %collective-permute-start.17) | collective-permute-done | bytes 262176 | tf_op jit(solution)/shard_map/ppermute | solution.py:20
  46.5 3.9 %collective-permute-done.16.refs_4_ = bf16[32,4096]{1,0:T(8,128)(2,1)S(1)} collective-permute-done((bf16[32,4096]{1,0:T(8,128)(2,1)}, bf16[32,4096]{1,0:T(8,128)(2,1)S(1)}, u32[]{:S(2)}, u32[]{:S(2)}) %collective-permute-start.16) | collective-permute-done | bytes 262176 | tf_op jit(solution)/shard_map/ppermute | solution.py:20
  50.5 0.9 %copy-done = bf16[32,4096]{1,0:T(8,128)(2,1)S(1)} copy-done((bf16[32,4096]{1,0:T(8,128)(2,1)S(1)}, bf16[32,4096]{1,0:T(8,128)(2,1)}, u32[]{:S(2)}) %copy-start) | copy-done | bytes 262168
  51.5 4.0 %update.1 = (f32[32,4096]{1,0:T(8,128)}, f32[128,128]{1,0:T(8,128)}) custom-call(f32[64,256]{1,0:T(8,128)S(1)} %add_add_fusion.refs_0_, f32[64,256]{1,0:T(8,128)S(1)} %collective-permute-done.14.refs_1_, bf16[32,4096]{1,0:T(8,128)(2,1)S(1)} %copy-done, bf16[32,4096]{1,0:T(8,128)(2,1)S(1)} %collective-permute-done.15.refs_3_, ...), custom_call_target="tpu_custom_call" | custom-call | tf_op jit(solution)/shard_map/update/pallas_call | solution.py:279
  (27 shorter events, 3.3 us)
Async XLA Ops:
  0.6 15.3 %copy-start.1 = (f32[32,512]{1,0:T(8,128)S(1)}, f32[32,512]{1,0:T(8,128)}, u32[]{:S(2)}) copy-start(f32[32,512]{1,0:T(8,128)} %refs_4_) | copy-start | bytes 196612
  0.6 28.8 %copy-start.3 = (f32[512]{0:T(512)S(1)}, f32[512]{0:T(512)}, u32[]{:S(2)}) copy-start(f32[512]{0:T(512)} %param.12) | copy-start | bytes 6148
  0.7 28.8 %copy-start.2 = (f32[512]{0:T(512)S(1)}, f32[512]{0:T(512)}, u32[]{:S(2)}) copy-start(f32[512]{0:T(512)} %param.11) | copy-start | bytes 6148
  7.4 1.9 %collective-permute-start = (f32[4,128,128]{2,1,0:T(8,128)}, f32[4,128,128]{2,1,0:T(8,128)S(1)}, u32[]{:S(2)}, u32[]{:S(2)}) collective-permute-start(f32[4,128,128]{2,1,0:T(8,128)} %get-tuple-element.13), channel_id=1, source_target_pairs={{0,4},{4,0},{1,5},{5,1},{2,6},{6,2},{3,7},{7,3},{8,12},{12,8},{9,1... | collective-permute-start | bytes 786440 | tf_op jit(solution)/shard_map/ppermute | solution.py:20
  10.4 8.8 %collective-permute-start.1 = (f32[128,128]{1,0:T(8,128)S(1)}, f32[128,128]{1,0:T(8,128)S(1)}, u32[]{:S(2)}, u32[]{:S(2)}) collective-permute-start(f32[128,128]{1,0:T(8,128)S(1)} %get-tuple-element.15), channel_id=1, source_target_pairs={{0,1},{1,0},{2,3},{3,2},{4,5},{5,4},{6,7},{7,6},{8,9},{9,8},{10,11... | collective-permute-start | bytes 196616 | tf_op jit(solution)/shard_map/ppermute | solution.py:20
  13.3 7.5 %collective-permute-start.2 = (f32[128,128]{1,0:T(8,128)S(1)}, f32[128,128]{1,0:T(8,128)S(1)}, u32[]{:S(2)}, u32[]{:S(2)}) collective-permute-start(f32[128,128]{1,0:T(8,128)S(1)} %get-tuple-element.16), channel_id=1, source_target_pairs={{0,2},{1,3},{2,0},{3,1},{4,6},{5,7},{6,4},{7,5},{8,10},{9,11},{10,... | collective-permute-start | bytes 196616 | tf_op jit(solution)/shard_map/ppermute | solution.py:20
  15.9 6.2 %collective-permute-start.3 = (f32[128,128]{1,0:T(8,128)S(1)}, f32[128,128]{1,0:T(8,128)S(1)}, u32[]{:S(2)}, u32[]{:S(2)}) collective-permute-start(f32[128,128]{1,0:T(8,128)S(1)} %get-tuple-element.17), channel_id=1, source_target_pairs={{0,3},{1,2},{2,1},{3,0},{4,7},{5,6},{6,5},{7,4},{8,11},{9,10},{10,... | collective-permute-start | bytes 196616 | tf_op jit(solution)/shard_map/ppermute | solution.py:20
  15.9 9.2 %collective-permute-start.9 = (f32[32,512]{1,0:T(8,128)S(1)}, f32[32,512]{1,0:T(8,128)S(1)}, u32[]{:S(2)}, u32[]{:S(2)}) collective-permute-start(f32[32,512]{1,0:T(8,128)S(1)} %copy-done.1), channel_id=1, source_target_pairs={{0,24},{8,16},{16,8},{24,0},{1,25},{9,17},{17,9},{25,1},{2,26},{10... | collective-permute-start | bytes 196616 | tf_op jit(solution)/shard_map/ppermute | solution.py:20
  18.6 7.1 %collective-permute-start.8 = (f32[32,512]{1,0:T(8,128)S(1)}, f32[32,512]{1,0:T(8,128)S(1)}, u32[]{:S(2)}, u32[]{:S(2)}) collective-permute-start(f32[32,512]{1,0:T(8,128)S(1)} %copy-done.1), channel_id=1, source_target_pairs={{0,16},{8,24},{16,0},{24,8},{1,17},{9,25},{17,1},{25,9},{2,18},{10... | collective-permute-start | bytes 196616 | tf_op jit(solution)/shard_map/ppermute | solution.py:20
  19.1 6.6 %collective-permute-start.7 = (f32[32,512]{1,0:T(8,128)S(1)}, f32[32,512]{1,0:T(8,128)S(1)}, u32[]{:S(2)}, u32[]{:S(2)}) collective-permute-start(f32[32,512]{1,0:T(8,128)S(1)} %copy-done.1), channel_id=1, source_target_pairs={{0,8},{8,0},{16,24},{24,16},{1,9},{9,1},{17,25},{25,17},{2,10},{10... | collective-permute-start | bytes 196616 | tf_op jit(solution)/shard_map/ppermute | solution.py:20
  22.1 5.9 %collective-permute-start.6 = (f32[128,128]{1,0:T(8,128)S(1)}, f32[128,128]{1,0:T(8,128)S(1)}, u32[]{:S(2)}, u32[]{:S(2)}) collective-permute-start(f32[128,128]{1,0:T(8,128)S(1)} %add_add_fusion.1.refs_0_), channel_id=1, source_target_pairs={{0,24},{8,16},{16,8},{24,0},{1,25},{9,17},{17,9},{25,1},{2,26},{10... | collective-permute-start | bytes 196616 | tf_op jit(solution)/shard_map/ppermute | solution.py:20
  24.7 4.3 %collective-permute-start.5 = (f32[128,128]{1,0:T(8,128)S(1)}, f32[128,128]{1,0:T(8,128)S(1)}, u32[]{:S(2)}, u32[]{:S(2)}) collective-permute-start(f32[128,128]{1,0:T(8,128)S(1)} %add_add_fusion.1.refs_0_), channel_id=1, source_target_pairs={{0,16},{8,24},{16,0},{24,8},{1,17},{9,25},{17,1},{25,9},{2,18},{10... | collective-permute-start | bytes 196616 | tf_op jit(solution)/shard_map/ppermute | solution.py:20
  25.2 4.3 %collective-permute-start.4 = (f32[128,128]{1,0:T(8,128)S(1)}, f32[128,128]{1,0:T(8,128)S(1)}, u32[]{:S(2)}, u32[]{:S(2)}) collective-permute-start(f32[128,128]{1,0:T(8,128)S(1)} %add_add_fusion.1.refs_0_), channel_id=1, source_target_pairs={{0,8},{8,0},{16,24},{24,16},{1,9},{9,1},{17,25},{25,17},{2,10},{10... | collective-permute-start | bytes 196616 | tf_op jit(solution)/shard_map/ppermute | solution.py:20
  30.4 1.3 %collective-permute-start.10 = (f32[64,256]{1,0:T(8,128)S(1)}, f32[64,256]{1,0:T(8,128)S(1)}, u32[]{:S(2)}, u32[]{:S(2)}) collective-permute-start(f32[64,256]{1,0:T(8,128)S(1)} %get-tuple-element.20), channel_id=1, source_target_pairs={{0,4},{4,0},{1,5},{5,1},{2,6},{6,2},{3,7},{7,3},{8,12},{12,8},{9,1... | collective-permute-start | bytes 196616 | tf_op jit(solution)/shard_map/ppermute | solution.py:20
  31.7 6.8 %collective-permute-start.13 = (f32[64,256]{1,0:T(8,128)S(1)}, f32[64,256]{1,0:T(8,128)S(1)}, u32[]{:S(2)}, u32[]{:S(2)}) collective-permute-start(f32[64,256]{1,0:T(8,128)S(1)} %add.56), channel_id=1, source_target_pairs={{0,3},{1,2},{2,1},{3,0},{4,7},{5,6},{6,5},{7,4},{8,11},{9,10},{10,... | collective-permute-start | bytes 196616 | tf_op jit(solution)/shard_map/ppermute | solution.py:20
  33.7 6.8 %collective-permute-start.12 = (f32[64,256]{1,0:T(8,128)S(1)}, f32[64,256]{1,0:T(8,128)S(1)}, u32[]{:S(2)}, u32[]{:S(2)}) collective-permute-start(f32[64,256]{1,0:T(8,128)S(1)} %add.56), channel_id=1, source_target_pairs={{0,2},{1,3},{2,0},{3,1},{4,6},{5,7},{6,4},{7,5},{8,10},{9,11},{10,... | collective-permute-start | bytes 196616 | tf_op jit(solution)/shard_map/ppermute | solution.py:20
  34.0 6.5 %collective-permute-start.11 = (f32[64,256]{1,0:T(8,128)S(1)}, f32[64,256]{1,0:T(8,128)S(1)}, u32[]{:S(2)}, u32[]{:S(2)}) collective-permute-start(f32[64,256]{1,0:T(8,128)S(1)} %add.56), channel_id=1, source_target_pairs={{0,1},{1,0},{2,3},{3,2},{4,5},{5,4},{6,7},{7,6},{8,9},{9,8},{10,11... | collective-permute-start | bytes 196616 | tf_op jit(solution)/shard_map/ppermute | solution.py:20
  36.1 10.3 %collective-permute-start.17 = (bf16[32,4096]{1,0:T(8,128)(2,1)}, bf16[32,4096]{1,0:T(8,128)(2,1)S(1)}, u32[]{:S(2)}, u32[]{:S(2)}) collective-permute-start(bf16[32,4096]{1,0:T(8,128)(2,1)} %get-tuple-element.21.refs_2_), channel_id=1, source_target_pairs={{0,24},{8,16},{16,8},{24,0},{1,25},{9,17},{17,9},{25,1},{2,26},{10... | collective-permute-start | bytes 786440 | tf_op jit(solution)/shard_map/ppermute | solution.py:20
  37.6 12.8 %collective-permute-start.16 = (bf16[32,4096]{1,0:T(8,128)(2,1)}, bf16[32,4096]{1,0:T(8,128)(2,1)S(1)}, u32[]{:S(2)}, u32[]{:S(2)}) collective-permute-start(bf16[32,4096]{1,0:T(8,128)(2,1)} %get-tuple-element.21.refs_2_), channel_id=1, source_target_pairs={{0,16},{8,24},{16,0},{24,8},{1,17},{9,25},{17,1},{25,9},{2,18},{10... | collective-permute-start | bytes 786440 | tf_op jit(solution)/shard_map/ppermute | solution.py:20
  38.5 12.0 %collective-permute-start.15 = (bf16[32,4096]{1,0:T(8,128)(2,1)}, bf16[32,4096]{1,0:T(8,128)(2,1)S(1)}, u32[]{:S(2)}, u32[]{:S(2)}) collective-permute-start(bf16[32,4096]{1,0:T(8,128)(2,1)} %get-tuple-element.21.refs_2_), channel_id=1, source_target_pairs={{0,8},{8,0},{16,24},{24,16},{1,9},{9,1},{17,25},{25,17},{2,10},{10... | collective-permute-start | bytes 786440 | tf_op jit(solution)/shard_map/ppermute | solution.py:20
  40.5 10.0 %collective-permute-start.14 = (f32[64,256]{1,0:T(8,128)S(1)}, f32[64,256]{1,0:T(8,128)S(1)}, u32[]{:S(2)}, u32[]{:S(2)}) collective-permute-start(f32[64,256]{1,0:T(8,128)S(1)} %add_add_fusion.refs_0_), channel_id=1, source_target_pairs={{0,4},{4,0},{1,5},{5,1},{2,6},{6,2},{3,7},{7,3},{8,12},{12,8},{9,1... | collective-permute-start | bytes 196616 | tf_op jit(solution)/shard_map/ppermute | solution.py:20
  50.5 1.0 %copy-start = (bf16[32,4096]{1,0:T(8,128)(2,1)S(1)}, bf16[32,4096]{1,0:T(8,128)(2,1)}, u32[]{:S(2)}) copy-start(bf16[32,4096]{1,0:T(8,128)(2,1)} %get-tuple-element.21.refs_2_) | copy-start | bytes 786436
where the time goes:
time: 55.7 us; the launch traced here: 55.4 us
  starting transfers between devices  20.9 us (38%)
  waiting for transfers between devices  20.2 us (36%)
  Pallas kernels  11.7 us (21%)
  other arithmetic  1.02 us (2%)
  local copies, waits for them, and re-layouts  0.96 us (2%)
  between operations  0.71 us (1%)
    ppermute x18, starting transfers between devices, swap(): return lax.ppermute(x, axis, [(i, i ^ distance) for i in range(size)])  20.9 us
    ppermute x18, waiting for transfers between devices, swap(): return lax.ppermute(x, axis, [(i, i ^ distance) for i in range(size)])  20.2 us
    pallas_call x1, Pallas kernels, contribute(): pl.pallas_call(functools.partial(contribute_kernel, owned, min(3, blocks)...  6.78 us
    pallas_call x1, Pallas kernels, update(): pl.pallas_call(functools.partial(update_kernel, count), in_specs=[VMEM, V...  3.97 us
  transfers between devices with their start and end apart: 18, of which 12 were waited for; matrix products, arithmetic and copies ran while one was open for 0% of the time, Pallas kernels for 0%

commit v1 on v0

--- a/solution.py
+++ b/solution.py
@@ -91,19 +91,26 @@
             copy.wait()
         rows = prior[:, cols(b)].astype(jnp.bfloat16)
         bf_ref[:, cols(b)] = rows
-        terms = lax.dot_general(
-            sens[b],
-            jnp.concatenate([rows] * copies, axis=0),
-            NT,
-            preferred_element_type=jnp.float32,
-        )
-        for k in range(slots):
-            block = pattern_ref[b, k]
-            at = storage[jnp.maximum(block, 0)]
-            group = jnp.where(block >= 0, (at % owned) // groups, -1)
-            acc[(at // owned) * groups + at % groups] += jnp.where(
-                lane_group == group, terms[k * obs_block : (k + 1) * obs_block], 0.0
+        rows = jnp.concatenate([rows] * copies, axis=0)
+
+        def add(count):
+            terms = lax.dot_general(
+                sens[b, : count * obs_block], rows, NT, preferred_element_type=jnp.float32
             )
+            for k in range(count):
+                block = pattern_ref[b, k]
+                at = storage[jnp.maximum(block, 0)]
+                group = jnp.where(block >= 0, (at % owned) // groups, -1)
+                acc[(at // owned) * groups + at % groups] += jnp.where(
+                    lane_group == group, terms[k * obs_block : (k + 1) * obs_block], 0.0
+                )
+
+        counts = list(range(slots // 4, slots + 1, 4))
+        for low, count in zip([0] + counts[:-1], counts):
+            fits = (low == 0) | (pattern_ref[b, low] >= 0)
+            if count < slots:
+                fits = fits & (pattern_ref[b, count] < 0)
+            pl.when(fits)(functools.partial(add, count))
         return carry
 
     lax.fori_loop(0, blocks, work, 0)
@@ -203,16 +210,18 @@
 def update_kernel(count, *refs):
     mine, other = refs[:2]
     prior = refs[2 : 2 + count]
-    increment, weights, both, cols, ensemble, sems = refs[2 + count :]
+    increment, weights, both, cols, ensemble, result, sems, out_sems = refs[2 + count :]
     members = weights.shape[0]
     members_dev = members // count
     at = lax.axis_index("member")
     side = lax.axis_index("slab")
     copies = []
-    for r in range(count):
+    for r in range(1, count):
         rows = pl.ds(pl.multiple_of((at ^ r) * members_dev, members_dev), members_dev)
         copies.append(pltpu.make_async_copy(prior[r], ensemble.at[rows, :], sems.at[r]))
         copies[-1].start()
+    own_rows = pl.ds(pl.multiple_of(at * members_dev, members_dev), members_dev)
+    ensemble[own_rows, :] = prior[0][...].astype(jnp.bfloat16)
     half = members // 2
     both[pl.ds(pl.multiple_of(side * half, half), half), :] = mine[...]
     both[pl.ds(pl.multiple_of((1 - side) * half, half), half), :] = other[...]
@@ -257,19 +266,20 @@
     weights[...] = terms
     centred = (terms - jnp.mean(terms, axis=0, keepdims=True)) * (1.0 / math.sqrt(members - 1))
     cols[...] = centred.T
-    own = cols[pl.ds(pl.multiple_of(at * members_dev, members_dev), members_dev), :].astype(
-        jnp.bfloat16
-    )
+    own = cols[own_rows, :].astype(jnp.bfloat16)
     for copy in copies:
         copy.wait()
-    width = 512
-
-    def multiply(n, carry):
-        lanes = pl.ds(pl.multiple_of(n * width, width), width)
-        increment[:, lanes] = jnp.dot(own, ensemble[:, lanes], preferred_element_type=jnp.float32)
-        return carry
-
-    lax.fori_loop(0, increment.shape[1] // width, multiply, 0, unroll=True)
+    outs = []
+    width = result.shape[1] // out_sems.shape[0]
+    for n in range(out_sems.shape[0]):
+        lanes = pl.ds(n * width, width)
+        result[:, lanes] = jnp.dot(own, ensemble[:, lanes], preferred_element_type=jnp.float32)
+        outs.append(
+            pltpu.make_async_copy(result.at[:, lanes], increment.at[:, lanes], out_sems.at[n])
+        )
+        outs[-1].start()
+    for copy in outs:
+        copy.wait()
 
 
 def update(mine, other, prior):
@@ -278,8 +288,8 @@
     members = members_dev * count
     return pl.pallas_call(
         functools.partial(update_kernel, count),
-        in_specs=[VMEM, VMEM] + [pl.BlockSpec(memory_space=pl.ANY)] * count,
-        out_specs=[VMEM, VMEM],
+        in_specs=[VMEM, VMEM, VMEM] + [pl.BlockSpec(memory_space=pl.ANY)] * (count - 1),
+        out_specs=[pl.BlockSpec(memory_space=pl.ANY), VMEM],
         out_shape=[
             jax.ShapeDtypeStruct((members_dev, params), jnp.float32),
             jax.ShapeDtypeStruct((members, members), jnp.float32),
@@ -288,7 +298,9 @@
             pltpu.VMEM((members, 2 * members), jnp.float32),
             pltpu.VMEM((members, members), jnp.float32),
             pltpu.VMEM((members, params), jnp.bfloat16),
+            pltpu.VMEM((members_dev, params), jnp.float32),
             pltpu.SemaphoreType.DMA((count,)),
+            pltpu.SemaphoreType.DMA((4,)),
         ],
         compiler_params=pltpu.CompilerParams(vmem_limit_bytes=8 << 20),
         name="update",
@@ -303,7 +315,7 @@
     chunks = [keep[r] + got[r] for r in range(tiles)]
     chunks, perturbation = lax.optimization_barrier((chunks, perturbation))
     noise = gather_xor(perturbation, "member")
-    ensemble = gather_xor(prior_bf, "member")
+    ensemble = [prior] + gather_xor(prior_bf, "member")[1:]
     for shift, radix in digits(tiles):
         low = 1 << shift
         arrived = [

time: 55.7 us -> 55.1 us (0.989)
  local copies, waits for them, and re-layouts: 0.96 us -> 0.02 us
    unnamed x8, local copies, waits for them, and re-layouts: 0.96 us -> 0.02 us
where the time goes in v1:
time: 55.1 us; the launch traced here: 54.8 us
  starting transfers between devices  20.8 us (38%)
  waiting for transfers between devices  20.1 us (36%)
  Pallas kernels  12.2 us (22%)
  other arithmetic  1.02 us (2%)
  between operations  0.71 us (1%)
    ppermute x18, starting transfers between devices, swap(): return lax.ppermute(x, axis, [(i, i ^ distance) for i in range(size)])  20.8 us
    ppermute x18, waiting for transfers between devices, swap(): return lax.ppermute(x, axis, [(i, i ^ distance) for i in range(size)])  20.1 us
    pallas_call x1, Pallas kernels, contribute(): pl.pallas_call(functools.partial(contribute_kernel, owned, min(3, blocks)...  6.76 us
    pallas_call x1, Pallas kernels, update(): pl.pallas_call(functools.partial(update_kernel, count), in_specs=[VMEM, V...  4.49 us
  transfers between devices with their start and end apart: 18, of which 12 were waited for; matrix products, arithmetic and copies ran while one was open for 0% of the time, Pallas kernels for 0%

profile of v1, /device:TPU:0, one launch (start us, length us, event | category | flops | bytes accessed | tf_op | source)
XLA Modules:
  0.0 54.8 jit_solution(1743748933369241133)
XLA Ops:
  0.7 6.8 %contribute.1 = (f32[4,128,128]{2,1,0:T(8,128)}, f32[4,128,128]{2,1,0:T(8,128)}, bf16[32,4096]{1,0:T(8,128)(2,1)}) custom-call(s32[8,16]{1,0:T(8,128)} %pattern_ref.1, s32[64]{0:T(128)} %ownership_ref.1, f32[32,4096]{1,0:T(8,128)} %refs_2_.1, bf16[8,1024,512]{2,1,0:T(8,128)(2,1)} %bitcast.13), custom_call_target="tpu_custom_call" | custom-call | tf_op jit(solution)/shard_map/contribute/pallas_call | solution.py:137
  7.9 1.4 %collective-permute-done = f32[4,128,128]{2,1,0:T(8,128)S(1)} collective-permute-done((f32[4,128,128]{2,1,0:T(8,128)}, f32[4,128,128]{2,1,0:T(8,128)S(1)}, u32[]{:S(2)}, u32[]{:S(2)}) %collective-permute-start) | collective-permute-done | bytes 262176 | tf_op jit(solution)/shard_map/ppermute | solution.py:20
  9.3 1.0 %fusion = (f32[128,128]{1,0:T(8,128)S(1)}, f32[128,128]{1,0:T(8,128)S(1)}, f32[128,128]{1,0:T(8,128)S(1)}, f32[128,128]{1,0:T(8,128)S(1)}) fusion(f32[4,128,128]{2,1,0:T(8,128)S(1)} %collective-permute-done, f32[4,128,128]{2,1,0:T(8,128)} %get-tuple-element.12), kind=kLoop, calls=%fused_computation.1 | loop fusion | flops 65536 | bytes 786432 | tf_op jit(solution)/shard_map/add | solution.py:315
  10.2 3.2 %collective-permute-start.1 = (f32[128,128]{1,0:T(8,128)S(1)}, f32[128,128]{1,0:T(8,128)S(1)}, u32[]{:S(2)}, u32[]{:S(2)}) collective-permute-start(f32[128,128]{1,0:T(8,128)S(1)} %get-tuple-element.15), channel_id=1, source_target_pairs={{0,1},{1,0},{2,3},{3,2},{4,5},{5,4},{6,7},{7,6},{8,9},{9,8},{10,11... | collective-permute-start | bytes 196616 | tf_op jit(solution)/shard_map/ppermute | solution.py:20
  13.4 2.4 %collective-permute-start.2 = (f32[128,128]{1,0:T(8,128)S(1)}, f32[128,128]{1,0:T(8,128)S(1)}, u32[]{:S(2)}, u32[]{:S(2)}) collective-permute-start(f32[128,128]{1,0:T(8,128)S(1)} %get-tuple-element.16), channel_id=1, source_target_pairs={{0,2},{1,3},{2,0},{3,1},{4,6},{5,7},{6,4},{7,5},{8,10},{9,11},{10,... | collective-permute-start | bytes 196616 | tf_op jit(solution)/shard_map/ppermute | solution.py:20
  15.8 2.7 %collective-permute-start.9 = (f32[32,512]{1,0:T(8,128)S(1)}, f32[32,512]{1,0:T(8,128)S(1)}, u32[]{:S(2)}, u32[]{:S(2)}) collective-permute-start(f32[32,512]{1,0:T(8,128)S(1)} %copy-done.1), channel_id=1, source_target_pairs={{0,24},{8,16},{16,8},{24,0},{1,25},{9,17},{17,9},{25,1},{2,26},{10... | collective-permute-start | bytes 196616 | tf_op jit(solution)/shard_map/ppermute | solution.py:20
  19.3 1.5 %collective-permute-done.2 = f32[128,128]{1,0:T(8,128)S(1)} collective-permute-done((f32[128,128]{1,0:T(8,128)S(1)}, f32[128,128]{1,0:T(8,128)S(1)}, u32[]{:S(2)}, u32[]{:S(2)}) %collective-permute-start.2) | collective-permute-done | bytes 65568 | tf_op jit(solution)/shard_map/ppermute | solution.py:20
  20.9 1.1 %collective-permute-done.3 = f32[128,128]{1,0:T(8,128)S(1)} collective-permute-done((f32[128,128]{1,0:T(8,128)S(1)}, f32[128,128]{1,0:T(8,128)S(1)}, u32[]{:S(2)}, u32[]{:S(2)}) %collective-permute-start.3) | collective-permute-done | bytes 65568 | tf_op jit(solution)/shard_map/ppermute | solution.py:20
  22.0 2.5 %collective-permute-start.6 = (f32[128,128]{1,0:T(8,128)S(1)}, f32[128,128]{1,0:T(8,128)S(1)}, u32[]{:S(2)}, u32[]{:S(2)}) collective-permute-start(f32[128,128]{1,0:T(8,128)S(1)} %add_add_fusion.1.refs_0_), channel_id=1, source_target_pairs={{0,24},{8,16},{16,8},{24,0},{1,25},{9,17},{17,9},{25,1},{2,26},{10... | collective-permute-start | bytes 196616 | tf_op jit(solution)/shard_map/ppermute | solution.py:20
  25.0 0.5 collective-permute-start.4
  25.5 2.3 %collective-permute-done.6.refs_3_ = f32[128,128]{1,0:T(8,128)S(1)} collective-permute-done((f32[128,128]{1,0:T(8,128)S(1)}, f32[128,128]{1,0:T(8,128)S(1)}, u32[]{:S(2)}, u32[]{:S(2)}) %collective-permute-start.6) | collective-permute-done | bytes 65568 | tf_op jit(solution)/shard_map/ppermute | solution.py:20
  27.8 0.9 %collective-permute-done.5.refs_2_ = f32[128,128]{1,0:T(8,128)S(1)} collective-permute-done((f32[128,128]{1,0:T(8,128)S(1)}, f32[128,128]{1,0:T(8,128)S(1)}, u32[]{:S(2)}, u32[]{:S(2)}) %collective-permute-start.5) | collective-permute-done | bytes 65568 | tf_op jit(solution)/shard_map/ppermute | solution.py:20
  29.3 0.9 %gram.1 = (f32[64,256]{1,0:T(8,128)S(1)}, f32[64,256]{1,0:T(8,128)S(1)}) custom-call(f32[128,128]{1,0:T(8,128)S(1)} %add_add_fusion.1.refs_0_, f32[128,128]{1,0:T(8,128)S(1)} %collective-permute-done.4.refs_1_, f32[128,128]{1,0:T(8,128)S(1)} %collective-permute-done.5.refs_2_, f32[128,128]{1,0:T(8,128)S(1)} %collective-permute-done.6.refs_3_, ...), custom_call_target="tpu_custom_call" | custom-call | tf_op jit(solution)/shard_map/gram/pallas_call | solution.py:196
  30.3 1.2 %collective-permute-done.10 = f32[64,256]{1,0:T(8,128)S(1)} collective-permute-done((f32[64,256]{1,0:T(8,128)S(1)}, f32[64,256]{1,0:T(8,128)S(1)}, u32[]{:S(2)}, u32[]{:S(2)}) %collective-permute-start.10) | collective-permute-done | bytes 65568 | tf_op jit(solution)/shard_map/ppermute | solution.py:20
  31.5 2.0 %collective-permute-start.13 = (f32[64,256]{1,0:T(8,128)S(1)}, f32[64,256]{1,0:T(8,128)S(1)}, u32[]{:S(2)}, u32[]{:S(2)}) collective-permute-start(f32[64,256]{1,0:T(8,128)S(1)} %add.56), channel_id=1, source_target_pairs={{0,3},{1,2},{2,1},{3,0},{4,7},{5,6},{6,5},{7,4},{8,11},{9,10},{10,... | collective-permute-start | bytes 196616 | tf_op jit(solution)/shard_map/ppermute | solution.py:20
  33.5 0.5 collective-permute-start.12
  34.0 2.0 %collective-permute-start.11 = (f32[64,256]{1,0:T(8,128)S(1)}, f32[64,256]{1,0:T(8,128)S(1)}, u32[]{:S(2)}, u32[]{:S(2)}) collective-permute-start(f32[64,256]{1,0:T(8,128)S(1)} %add.56), channel_id=1, source_target_pairs={{0,1},{1,0},{2,3},{3,2},{4,5},{5,4},{6,7},{7,6},{8,9},{9,8},{10,11... | collective-permute-start | bytes 196616 | tf_op jit(solution)/shard_map/ppermute | solution.py:20
  36.0 1.5 %collective-permute-start.17 = (bf16[32,4096]{1,0:T(8,128)(2,1)}, bf16[32,4096]{1,0:T(8,128)(2,1)S(1)}, u32[]{:S(2)}, u32[]{:S(2)}) collective-permute-start(bf16[32,4096]{1,0:T(8,128)(2,1)} %get-tuple-element.21), channel_id=1, source_target_pairs={{0,24},{8,16},{16,8},{24,0},{1,25},{9,17},{17,9},{25,1},{2,26},{10... | collective-permute-start | bytes 786440 | tf_op jit(solution)/shard_map/ppermute | solution.py:20
  37.5 0.5 collective-permute-start.16
  38.4 1.1 %collective-permute-start.15 = (bf16[32,4096]{1,0:T(8,128)(2,1)}, bf16[32,4096]{1,0:T(8,128)(2,1)S(1)}, u32[]{:S(2)}, u32[]{:S(2)}) collective-permute-start(bf16[32,4096]{1,0:T(8,128)(2,1)} %get-tuple-element.21), channel_id=1, source_target_pairs={{0,8},{8,0},{16,24},{24,16},{1,9},{9,1},{17,25},{25,17},{2,10},{10... | collective-permute-start | bytes 786440 | tf_op jit(solution)/shard_map/ppermute | solution.py:20
  39.5 1.0 %collective-permute-done.12 = f32[64,256]{1,0:T(8,128)S(1)} collective-permute-done((f32[64,256]{1,0:T(8,128)S(1)}, f32[64,256]{1,0:T(8,128)S(1)}, u32[]{:S(2)}, u32[]{:S(2)}) %collective-permute-start.12) | collective-permute-done | bytes 65568 | tf_op jit(solution)/shard_map/ppermute | solution.py:20
  40.7 5.7 %collective-permute-done.17.refs_5_ = bf16[32,4096]{1,0:T(8,128)(2,1)S(1)} collective-permute-done((bf16[32,4096]{1,0:T(8,128)(2,1)}, bf16[32,4096]{1,0:T(8,128)(2,1)S(1)}, u32[]{:S(2)}, u32[]{:S(2)}) %collective-permute-start.17) | collective-permute-done | bytes 262176 | tf_op jit(solution)/shard_map/ppermute | solution.py:20
  46.3 3.9 %collective-permute-done.16.refs_4_ = bf16[32,4096]{1,0:T(8,128)(2,1)S(1)} collective-permute-done((bf16[32,4096]{1,0:T(8,128)(2,1)}, bf16[32,4096]{1,0:T(8,128)(2,1)S(1)}, u32[]{:S(2)}, u32[]{:S(2)}) %collective-permute-start.16) | collective-permute-done | bytes 262176 | tf_op jit(solution)/shard_map/ppermute | solution.py:20
  50.3 4.5 %update.1 = (f32[32,4096]{1,0:T(8,128)}, f32[128,128]{1,0:T(8,128)}) custom-call(f32[64,256]{1,0:T(8,128)S(1)} %add_add_fusion.refs_0_, f32[64,256]{1,0:T(8,128)S(1)} %collective-permute-done.14.refs_1_, f32[32,4096]{1,0:T(8,128)S(1)} %copy-done, bf16[32,4096]{1,0:T(8,128)(2,1)S(1)} %collective-permute-done.15.refs_3_, ...), custom_call_target="tpu_custom_call" | custom-call | tf_op jit(solution)/shard_map/update/pallas_call | solution.py:289
  (27 shorter events, 3.1 us)
Async XLA Ops:
  0.6 49.7 %copy-start = (f32[32,4096]{1,0:T(8,128)S(1)}, f32[32,4096]{1,0:T(8,128)}, u32[]{:S(2)}) copy-start(f32[32,4096]{1,0:T(8,128)} %refs_2_.1) | copy-start | bytes 1572868
  0.6 15.2 %copy-start.1 = (f32[32,512]{1,0:T(8,128)S(1)}, f32[32,512]{1,0:T(8,128)}, u32[]{:S(2)}) copy-start(f32[32,512]{1,0:T(8,128)} %refs_4_) | copy-start | bytes 196612
  0.7 28.6 %copy-start.3 = (f32[512]{0:T(512)S(1)}, f32[512]{0:T(512)}, u32[]{:S(2)}) copy-start(f32[512]{0:T(512)} %param.12) | copy-start | bytes 6148
  0.7 28.6 %copy-start.2 = (f32[512]{0:T(512)S(1)}, f32[512]{0:T(512)}, u32[]{:S(2)}) copy-start(f32[512]{0:T(512)} %param.11) | copy-start | bytes 6148
  7.4 1.8 %collective-permute-start = (f32[4,128,128]{2,1,0:T(8,128)}, f32[4,128,128]{2,1,0:T(8,128)S(1)}, u32[]{:S(2)}, u32[]{:S(2)}) collective-permute-start(f32[4,128,128]{2,1,0:T(8,128)} %get-tuple-element.13), channel_id=1, source_target_pairs={{0,4},{4,0},{1,5},{5,1},{2,6},{6,2},{3,7},{7,3},{8,12},{12,8},{9,1... | collective-permute-start | bytes 786440 | tf_op jit(solution)/shard_map/ppermute | solution.py:20
  10.2 8.9 %collective-permute-start.1 = (f32[128,128]{1,0:T(8,128)S(1)}, f32[128,128]{1,0:T(8,128)S(1)}, u32[]{:S(2)}, u32[]{:S(2)}) collective-permute-start(f32[128,128]{1,0:T(8,128)S(1)} %get-tuple-element.15), channel_id=1, source_target_pairs={{0,1},{1,0},{2,3},{3,2},{4,5},{5,4},{6,7},{7,6},{8,9},{9,8},{10,11... | collective-permute-start | bytes 196616 | tf_op jit(solution)/shard_map/ppermute | solution.py:20
  13.4 7.5 %collective-permute-start.2 = (f32[128,128]{1,0:T(8,128)S(1)}, f32[128,128]{1,0:T(8,128)S(1)}, u32[]{:S(2)}, u32[]{:S(2)}) collective-permute-start(f32[128,128]{1,0:T(8,128)S(1)} %get-tuple-element.16), channel_id=1, source_target_pairs={{0,2},{1,3},{2,0},{3,1},{4,6},{5,7},{6,4},{7,5},{8,10},{9,11},{10,... | collective-permute-start | bytes 196616 | tf_op jit(solution)/shard_map/ppermute | solution.py:20
  15.8 6.2 %collective-permute-start.3 = (f32[128,128]{1,0:T(8,128)S(1)}, f32[128,128]{1,0:T(8,128)S(1)}, u32[]{:S(2)}, u32[]{:S(2)}) collective-permute-start(f32[128,128]{1,0:T(8,128)S(1)} %get-tuple-element.17), channel_id=1, source_target_pairs={{0,3},{1,2},{2,1},{3,0},{4,7},{5,6},{6,5},{7,4},{8,11},{9,10},{10,... | collective-permute-start | bytes 196616 | tf_op jit(solution)/shard_map/ppermute | solution.py:20
  15.8 9.1 %collective-permute-start.9 = (f32[32,512]{1,0:T(8,128)S(1)}, f32[32,512]{1,0:T(8,128)S(1)}, u32[]{:S(2)}, u32[]{:S(2)}) collective-permute-start(f32[32,512]{1,0:T(8,128)S(1)} %copy-done.1), channel_id=1, source_target_pairs={{0,24},{8,16},{16,8},{24,0},{1,25},{9,17},{17,9},{25,1},{2,26},{10... | collective-permute-start | bytes 196616 | tf_op jit(solution)/shard_map/ppermute | solution.py:20
  18.6 7.0 %collective-permute-start.8 = (f32[32,512]{1,0:T(8,128)S(1)}, f32[32,512]{1,0:T(8,128)S(1)}, u32[]{:S(2)}, u32[]{:S(2)}) collective-permute-start(f32[32,512]{1,0:T(8,128)S(1)} %copy-done.1), channel_id=1, source_target_pairs={{0,16},{8,24},{16,0},{24,8},{1,17},{9,25},{17,1},{25,9},{2,18},{10... | collective-permute-start | bytes 196616 | tf_op jit(solution)/shard_map/ppermute | solution.py:20
  19.1 6.4 %collective-permute-start.7 = (f32[32,512]{1,0:T(8,128)S(1)}, f32[32,512]{1,0:T(8,128)S(1)}, u32[]{:S(2)}, u32[]{:S(2)}) collective-permute-start(f32[32,512]{1,0:T(8,128)S(1)} %copy-done.1), channel_id=1, source_target_pairs={{0,8},{8,0},{16,24},{24,16},{1,9},{9,1},{17,25},{25,17},{2,10},{10... | collective-permute-start | bytes 196616 | tf_op jit(solution)/shard_map/ppermute | solution.py:20
  22.0 5.8 %collective-permute-start.6 = (f32[128,128]{1,0:T(8,128)S(1)}, f32[128,128]{1,0:T(8,128)S(1)}, u32[]{:S(2)}, u32[]{:S(2)}) collective-permute-start(f32[128,128]{1,0:T(8,128)S(1)} %add_add_fusion.1.refs_0_), channel_id=1, source_target_pairs={{0,24},{8,16},{16,8},{24,0},{1,25},{9,17},{17,9},{25,1},{2,26},{10... | collective-permute-start | bytes 196616 | tf_op jit(solution)/shard_map/ppermute | solution.py:20
  24.5 4.3 %collective-permute-start.5 = (f32[128,128]{1,0:T(8,128)S(1)}, f32[128,128]{1,0:T(8,128)S(1)}, u32[]{:S(2)}, u32[]{:S(2)}) collective-permute-start(f32[128,128]{1,0:T(8,128)S(1)} %add_add_fusion.1.refs_0_), channel_id=1, source_target_pairs={{0,16},{8,24},{16,0},{24,8},{1,17},{9,25},{17,1},{25,9},{2,18},{10... | collective-permute-start | bytes 196616 | tf_op jit(solution)/shard_map/ppermute | solution.py:20
  25.0 4.3 %collective-permute-start.4 = (f32[128,128]{1,0:T(8,128)S(1)}, f32[128,128]{1,0:T(8,128)S(1)}, u32[]{:S(2)}, u32[]{:S(2)}) collective-permute-start(f32[128,128]{1,0:T(8,128)S(1)} %add_add_fusion.1.refs_0_), channel_id=1, source_target_pairs={{0,8},{8,0},{16,24},{24,16},{1,9},{9,1},{17,25},{25,17},{2,10},{10... | collective-permute-start | bytes 196616 | tf_op jit(solution)/shard_map/ppermute | solution.py:20
  30.2 1.3 %collective-permute-start.10 = (f32[64,256]{1,0:T(8,128)S(1)}, f32[64,256]{1,0:T(8,128)S(1)}, u32[]{:S(2)}, u32[]{:S(2)}) collective-permute-start(f32[64,256]{1,0:T(8,128)S(1)} %get-tuple-element.20), channel_id=1, source_target_pairs={{0,4},{4,0},{1,5},{5,1},{2,6},{6,2},{3,7},{7,3},{8,12},{12,8},{9,1... | collective-permute-start | bytes 196616 | tf_op jit(solution)/shard_map/ppermute | solution.py:20
  31.5 6.9 %collective-permute-start.13 = (f32[64,256]{1,0:T(8,128)S(1)}, f32[64,256]{1,0:T(8,128)S(1)}, u32[]{:S(2)}, u32[]{:S(2)}) collective-permute-start(f32[64,256]{1,0:T(8,128)S(1)} %add.56), channel_id=1, source_target_pairs={{0,3},{1,2},{2,1},{3,0},{4,7},{5,6},{6,5},{7,4},{8,11},{9,10},{10,... | collective-permute-start | bytes 196616 | tf_op jit(solution)/shard_map/ppermute | solution.py:20
  33.5 7.0 %collective-permute-start.12 = (f32[64,256]{1,0:T(8,128)S(1)}, f32[64,256]{1,0:T(8,128)S(1)}, u32[]{:S(2)}, u32[]{:S(2)}) collective-permute-start(f32[64,256]{1,0:T(8,128)S(1)} %add.56), channel_id=1, source_target_pairs={{0,2},{1,3},{2,0},{3,1},{4,6},{5,7},{6,4},{7,5},{8,10},{9,11},{10,... | collective-permute-start | bytes 196616 | tf_op jit(solution)/shard_map/ppermute | solution.py:20
  34.0 6.5 %collective-permute-start.11 = (f32[64,256]{1,0:T(8,128)S(1)}, f32[64,256]{1,0:T(8,128)S(1)}, u32[]{:S(2)}, u32[]{:S(2)}) collective-permute-start(f32[64,256]{1,0:T(8,128)S(1)} %add.56), channel_id=1, source_target_pairs={{0,1},{1,0},{2,3},{3,2},{4,5},{5,4},{6,7},{7,6},{8,9},{9,8},{10,11... | collective-permute-start | bytes 196616 | tf_op jit(solution)/shard_map/ppermute | solution.py:20
  36.0 10.3 %collective-permute-start.17 = (bf16[32,4096]{1,0:T(8,128)(2,1)}, bf16[32,4096]{1,0:T(8,128)(2,1)S(1)}, u32[]{:S(2)}, u32[]{:S(2)}) collective-permute-start(bf16[32,4096]{1,0:T(8,128)(2,1)} %get-tuple-element.21), channel_id=1, source_target_pairs={{0,24},{8,16},{16,8},{24,0},{1,25},{9,17},{17,9},{25,1},{2,26},{10... | collective-permute-start | bytes 786440 | tf_op jit(solution)/shard_map/ppermute | solution.py:20
  37.5 12.8 %collective-permute-start.16 = (bf16[32,4096]{1,0:T(8,128)(2,1)}, bf16[32,4096]{1,0:T(8,128)(2,1)S(1)}, u32[]{:S(2)}, u32[]{:S(2)}) collective-permute-start(bf16[32,4096]{1,0:T(8,128)(2,1)} %get-tuple-element.21), channel_id=1, source_target_pairs={{0,16},{8,24},{16,0},{24,8},{1,17},{9,25},{17,1},{25,9},{2,18},{10... | collective-permute-start | bytes 786440 | tf_op jit(solution)/shard_map/ppermute | solution.py:20
  38.4 11.9 %collective-permute-start.15 = (bf16[32,4096]{1,0:T(8,128)(2,1)}, bf16[32,4096]{1,0:T(8,128)(2,1)S(1)}, u32[]{:S(2)}, u32[]{:S(2)}) collective-permute-start(bf16[32,4096]{1,0:T(8,128)(2,1)} %get-tuple-element.21), channel_id=1, source_target_pairs={{0,8},{8,0},{16,24},{24,16},{1,9},{9,1},{17,25},{25,17},{2,10},{10... | collective-permute-start | bytes 786440 | tf_op jit(solution)/shard_map/ppermute | solution.py:20
  40.5 9.8 %collective-permute-start.14 = (f32[64,256]{1,0:T(8,128)S(1)}, f32[64,256]{1,0:T(8,128)S(1)}, u32[]{:S(2)}, u32[]{:S(2)}) collective-permute-start(f32[64,256]{1,0:T(8,128)S(1)} %add_add_fusion.refs_0_), channel_id=1, source_target_pairs={{0,4},{4,0},{1,5},{5,1},{2,6},{6,2},{3,7},{7,3},{8,12},{12,8},{9,1... | collective-permute-start | bytes 196616 | tf_op jit(solution)/shard_map/ppermute | solution.py:20

commit v2 on v1

--- a/solution.py
+++ b/solution.py
@@ -181,18 +181,30 @@
     )
     row = lax.broadcasted_iota(jnp.int32, both.shape, 0)
     col = lax.broadcasted_iota(jnp.int32, both.shape, 1)
-    whole[...] = both + jnp.where(row == col, misfit * (1.0 / (4.0 * members * members)), 0.0)
-    rows = members // 2
+    both = both + jnp.where(row == col, misfit * (1.0 / (4.0 * members * members)), 0.0)
+    system, cross = both[:, :members], both[:, members:]
+    half = members // 2
+    first, last = system[:half, :half], system[half:, half:]
+    above = row[:half, :half] <= col[:half, :half]
+    whole[: members, :] = cross
+    whole[members : members + half, :half] = system[:half, half:]
+    whole[members : members + half, half:] = jnp.where(above, first, last)
+    diagonal = jnp.sum(jnp.where(row == col, both, 0.0)[:, :members], axis=0, keepdims=True)
     side = lax.axis_index("slab")
-    keep[...] = whole[pl.ds(pl.multiple_of(side * rows, rows), rows), :]
-    send[...] = whole[pl.ds(pl.multiple_of((1 - side) * rows, rows), rows), :]
+    for out, at in ((keep, side), (send, 1 - side)):
+        out[:half, :] = whole[pl.ds(pl.multiple_of(at * half, half), half), :]
+        quarter = half // 2
+        out[half : half + quarter, :] = whole[
+            pl.ds(pl.multiple_of(members + at * quarter, quarter), quarter), :
+        ]
+        out[half + quarter :, :] = jnp.broadcast_to(diagonal, (8, members))
 
 
 def gram(predicted, noise, observed, sigma):
     count = len(predicted)
     members_dev, obs_dev = noise[0].shape
     members = members_dev * count
-    half = jax.ShapeDtypeStruct((members // 2, 2 * members), jnp.float32)
+    half = jax.ShapeDtypeStruct((members // 2 + members // 4 + 8, members), jnp.float32)
     return pl.pallas_call(
         functools.partial(gram_kernel, count),
         in_specs=[VMEM] * (2 * count + 2),
@@ -200,7 +212,7 @@
         out_shape=[half, half],
         scratch_shapes=[
             pltpu.VMEM((2 * members, obs_dev), jnp.float32),
-            pltpu.VMEM((members, 2 * members), jnp.float32),
+            pltpu.VMEM((members + members // 2, members), jnp.float32),
         ],
         compiler_params=pltpu.CompilerParams(vmem_limit_bytes=8 << 20),
         name="gram",
@@ -210,35 +222,48 @@
 def update_kernel(count, *refs):
     mine, other = refs[:2]
     prior = refs[2 : 2 + count]
-    increment, weights, both, cols, ensemble, result, sems, out_sems = refs[2 + count :]
+    increment, weights, cross, packed, cols, ensemble, _, _ = refs[2 + count :]
     members = weights.shape[0]
     members_dev = members // count
     at = lax.axis_index("member")
     side = lax.axis_index("slab")
-    copies = []
-    for r in range(1, count):
+    own_rows = pl.ds(pl.multiple_of(at * members_dev, members_dev), members_dev)
+    for r in range(count):
         rows = pl.ds(pl.multiple_of((at ^ r) * members_dev, members_dev), members_dev)
-        copies.append(pltpu.make_async_copy(prior[r], ensemble.at[rows, :], sems.at[r]))
-        copies[-1].start()
-    own_rows = pl.ds(pl.multiple_of(at * members_dev, members_dev), members_dev)
-    ensemble[own_rows, :] = prior[0][...].astype(jnp.bfloat16)
-    half = members // 2
-    both[pl.ds(pl.multiple_of(side * half, half), half), :] = mine[...]
-    both[pl.ds(pl.multiple_of((1 - side) * half, half), half), :] = other[...]
+        ensemble[rows, :] = prior[r][...].astype(jnp.bfloat16)
+    half, quarter = members // 2, members // 4
+    for part, at_side in ((mine, side), (other, 1 - side)):
+        cross[pl.ds(pl.multiple_of(at_side * half, half), half), :] = part[:half, :]
+        packed[pl.ds(pl.multiple_of(at_side * quarter, quarter), quarter), :] = part[
+            half : half + quarter, :
+        ]
     row = lax.broadcasted_iota(jnp.int32, (members, members), 0)
     col = lax.broadcasted_iota(jnp.int32, (members, members), 1)
     eye = jnp.where(row == col, 1.0, 0.0)
-    system = both[:, :members]
+    top = packed[...]
+    turned = top.T
+    mixed, mixed_turned = top[:, half:], turned[half:, :]
+    above = row[:half, :half] <= col[:half, :half]
+    system = jnp.concatenate(
+        [
+            jnp.concatenate([jnp.where(above, mixed, mixed_turned), top[:, :half]], axis=1),
+            jnp.concatenate([turned[:half, :], jnp.where(above, mixed_turned, mixed)], axis=1),
+        ],
+        axis=0,
+    )
+    system = jnp.where(row == col, mine[half + quarter : half + quarter + 1, :], system)
 
     def total(x):
         return jnp.sum(jnp.sum(x, axis=0, keepdims=True), axis=1, keepdims=True)
 
     trace = total(system * eye)
-    system = system + trace * (1.0 / (members * members))
+    system = system + (trace - total(system)) * (1.0 / (members * members))
     bound = jnp.max(jnp.sum(jnp.abs(system), axis=0, keepdims=True), axis=1, keepdims=True)
-    scale = jnp.minimum(trace * (1.0 + 1.0 / members) / total(system * system), 1.9 / bound)
-    power = eye - scale * system
-    terms = both[:, members:] * scale
+
+    def begin(scale):
+        return eye - scale * system, cross[...] * scale
+
+    power, terms = begin(total(system * eye) / total(system * system))
 
     def step(power, terms):
         pair = lax.dot_general(
@@ -250,7 +275,7 @@
         )
         return pair[:, :members], terms + pair[:, members:]
 
-    for _ in range(5):
+    for _ in range(4):
         power, terms = step(power, terms)
 
     def unfinished(carry):
@@ -262,24 +287,19 @@
         power, terms = step(power, terms)
         return power, terms, count + 1
 
+    shrinks = jnp.sum(power * power, axis=0, keepdims=True)
+    shrinks = jnp.sum(shrinks, axis=1, keepdims=True) < 1.0
+    sure_power, sure_terms = begin(1.9 / bound)
+    power = jnp.where(shrinks, power, sure_power)
+    terms = jnp.where(shrinks, terms, sure_terms)
     _, terms, _ = lax.while_loop(unfinished, further, (power, terms, 0))
     weights[...] = terms
     centred = (terms - jnp.mean(terms, axis=0, keepdims=True)) * (1.0 / math.sqrt(members - 1))
     cols[...] = centred.T
     own = cols[own_rows, :].astype(jnp.bfloat16)
-    for copy in copies:
-        copy.wait()
-    outs = []
-    width = result.shape[1] // out_sems.shape[0]
-    for n in range(out_sems.shape[0]):
-        lanes = pl.ds(n * width, width)
-        result[:, lanes] = jnp.dot(own, ensemble[:, lanes], preferred_element_type=jnp.float32)
-        outs.append(
-            pltpu.make_async_copy(result.at[:, lanes], increment.at[:, lanes], out_sems.at[n])
-        )
-        outs[-1].start()
-    for copy in outs:
-        copy.wait()
+    for n in range(4):
+        lanes = pl.ds(n * 1024, 1024)
+        increment[:, lanes] = jnp.dot(own, ensemble[:, lanes], preferred_element_type=jnp.float32)
 
 
 def update(mine, other, prior):
@@ -288,18 +308,18 @@
     members = members_dev * count
     return pl.pallas_call(
         functools.partial(update_kernel, count),
-        in_specs=[VMEM, VMEM, VMEM] + [pl.BlockSpec(memory_space=pl.ANY)] * (count - 1),
-        out_specs=[pl.BlockSpec(memory_space=pl.ANY), VMEM],
+        in_specs=[VMEM] * (2 + count),
+        out_specs=[VMEM, VMEM],
         out_shape=[
             jax.ShapeDtypeStruct((members_dev, params), jnp.float32),
             jax.ShapeDtypeStruct((members, members), jnp.float32),
         ],
         scratch_shapes=[
-            pltpu.VMEM((members, 2 * members), jnp.float32),
+            pltpu.VMEM((members, members), jnp.float32),
+            pltpu.VMEM((members // 2, members), jnp.float32),
             pltpu.VMEM((members, members), jnp.float32),
             pltpu.VMEM((members, params), jnp.bfloat16),
             pltpu.VMEM((members_dev, params), jnp.float32),
-            pltpu.SemaphoreType.DMA((count,)),
             pltpu.SemaphoreType.DMA((4,)),
         ],
         compiler_params=pltpu.CompilerParams(vmem_limit_bytes=8 << 20),

time: 55.1 us -> 56.6 us (1.027)
  Pallas kernels: 12.2 us -> 13.8 us
    pallas_call x1, Pallas kernels: 4.49 us -> 5.96 us  [update(): pl.pallas_call(functools.partial(update_kernel, count), in_specs=[VMEM] *...]
  transfers between devices with their start and end apart: 18 -> 18, of which waited for: 12 -> 11; matrix products, arithmetic and copies ran while one was open for 0% -> 0% of each run, Pallas kernels for 0% -> 0%
where the time goes in v2:
time: 56.6 us; the launch traced here: 56.4 us
  starting transfers between devices  21.2 us (37%)
  waiting for transfers between devices  19.6 us (35%)
  Pallas kernels  13.8 us (24%)
  other arithmetic  1.02 us (2%)
  between operations  0.71 us (1%)
    ppermute x18, starting transfers between devices, swap(): return lax.ppermute(x, axis, [(i, i ^ distance) for i in range(size)])  21.2 us
    ppermute x18, waiting for transfers between devices, swap(): return lax.ppermute(x, axis, [(i, i ^ distance) for i in range(size)])  19.6 us
    pallas_call x1, Pallas kernels, contribute(): pl.pallas_call(functools.partial(contribute_kernel, owned, min(3, blocks)...  6.76 us
    pallas_call x1, Pallas kernels, update(): pl.pallas_call(functools.partial(update_kernel, count), in_specs=[VMEM] *...  5.96 us
  transfers between devices with their start and end apart: 18, of which 11 were waited for; matrix products, arithmetic and copies ran while one was open for 0% of the time, Pallas kernels for 0%

profile of v2, /device:TPU:0, one launch (start us, length us, event | category | flops | bytes accessed | tf_op | source)
XLA Modules:
  0.0 56.4 jit_solution(8682366405911037019)
XLA Ops:
  0.7 6.8 %contribute.1 = (f32[4,128,128]{2,1,0:T(8,128)}, f32[4,128,128]{2,1,0:T(8,128)}, bf16[32,4096]{1,0:T(8,128)(2,1)}) custom-call(s32[8,16]{1,0:T(8,128)} %pattern_ref.1, s32[64]{0:T(128)} %ownership_ref.1, f32[32,4096]{1,0:T(8,128)} %refs_2_.1, bf16[8,1024,512]{2,1,0:T(8,128)(2,1)} %bitcast.13), custom_call_target="tpu_custom_call" | custom-call | tf_op jit(solution)/shard_map/contribute/pallas_call | solution.py:137
  7.9 1.4 %collective-permute-done = f32[4,128,128]{2,1,0:T(8,128)S(1)} collective-permute-done((f32[4,128,128]{2,1,0:T(8,128)}, f32[4,128,128]{2,1,0:T(8,128)S(1)}, u32[]{:S(2)}, u32[]{:S(2)}) %collective-permute-start) | collective-permute-done | bytes 262176 | tf_op jit(solution)/shard_map/ppermute | solution.py:20
  9.3 1.0 %fusion = (f32[128,128]{1,0:T(8,128)S(1)}, f32[128,128]{1,0:T(8,128)S(1)}, f32[128,128]{1,0:T(8,128)S(1)}, f32[128,128]{1,0:T(8,128)S(1)}) fusion(f32[4,128,128]{2,1,0:T(8,128)S(1)} %collective-permute-done, f32[4,128,128]{2,1,0:T(8,128)} %get-tuple-element.12), kind=kLoop, calls=%fused_computation.1 | loop fusion | flops 65536 | bytes 786432 | tf_op jit(solution)/shard_map/add | solution.py:335
  10.2 3.2 %collective-permute-start.1 = (f32[128,128]{1,0:T(8,128)S(1)}, f32[128,128]{1,0:T(8,128)S(1)}, u32[]{:S(2)}, u32[]{:S(2)}) collective-permute-start(f32[128,128]{1,0:T(8,128)S(1)} %get-tuple-element.15), channel_id=1, source_target_pairs={{0,1},{1,0},{2,3},{3,2},{4,5},{5,4},{6,7},{7,6},{8,9},{9,8},{10,11... | collective-permute-start | bytes 196616 | tf_op jit(solution)/shard_map/ppermute | solution.py:20
  13.4 2.4 %collective-permute-start.2 = (f32[128,128]{1,0:T(8,128)S(1)}, f32[128,128]{1,0:T(8,128)S(1)}, u32[]{:S(2)}, u32[]{:S(2)}) collective-permute-start(f32[128,128]{1,0:T(8,128)S(1)} %get-tuple-element.16), channel_id=1, source_target_pairs={{0,2},{1,3},{2,0},{3,1},{4,6},{5,7},{6,4},{7,5},{8,10},{9,11},{10,... | collective-permute-start | bytes 196616 | tf_op jit(solution)/shard_map/ppermute | solution.py:20
  15.8 2.7 %collective-permute-start.9 = (f32[32,512]{1,0:T(8,128)S(1)}, f32[32,512]{1,0:T(8,128)S(1)}, u32[]{:S(2)}, u32[]{:S(2)}) collective-permute-start(f32[32,512]{1,0:T(8,128)S(1)} %copy-done.1), channel_id=1, source_target_pairs={{0,24},{8,16},{16,8},{24,0},{1,25},{9,17},{17,9},{25,1},{2,26},{10... | collective-permute-start | bytes 196616 | tf_op jit(solution)/shard_map/ppermute | solution.py:20
  18.6 0.5 collective-permute-start.8
  19.3 1.5 %collective-permute-done.2 = f32[128,128]{1,0:T(8,128)S(1)} collective-permute-done((f32[128,128]{1,0:T(8,128)S(1)}, f32[128,128]{1,0:T(8,128)S(1)}, u32[]{:S(2)}, u32[]{:S(2)}) %collective-permute-start.2) | collective-permute-done | bytes 65568 | tf_op jit(solution)/shard_map/ppermute | solution.py:20
  20.9 1.1 %collective-permute-done.3 = f32[128,128]{1,0:T(8,128)S(1)} collective-permute-done((f32[128,128]{1,0:T(8,128)S(1)}, f32[128,128]{1,0:T(8,128)S(1)}, u32[]{:S(2)}, u32[]{:S(2)}) %collective-permute-start.3) | collective-permute-done | bytes 65568 | tf_op jit(solution)/shard_map/ppermute | solution.py:20
  22.0 2.5 %collective-permute-start.6 = (f32[128,128]{1,0:T(8,128)S(1)}, f32[128,128]{1,0:T(8,128)S(1)}, u32[]{:S(2)}, u32[]{:S(2)}) collective-permute-start(f32[128,128]{1,0:T(8,128)S(1)} %add_add_fusion.refs_0_), channel_id=1, source_target_pairs={{0,24},{8,16},{16,8},{24,0},{1,25},{9,17},{17,9},{25,1},{2,26},{10... | collective-permute-start | bytes 196616 | tf_op jit(solution)/shard_map/ppermute | solution.py:20
  25.0 0.5 collective-permute-start.4
  25.5 2.3 %collective-permute-done.6.refs_3_ = f32[128,128]{1,0:T(8,128)S(1)} collective-permute-done((f32[128,128]{1,0:T(8,128)S(1)}, f32[128,128]{1,0:T(8,128)S(1)}, u32[]{:S(2)}, u32[]{:S(2)}) %collective-permute-start.6) | collective-permute-done | bytes 65568 | tf_op jit(solution)/shard_map/ppermute | solution.py:20
  27.8 0.9 %collective-permute-done.5.refs_2_ = f32[128,128]{1,0:T(8,128)S(1)} collective-permute-done((f32[128,128]{1,0:T(8,128)S(1)}, f32[128,128]{1,0:T(8,128)S(1)}, u32[]{:S(2)}, u32[]{:S(2)}) %collective-permute-start.5) | collective-permute-done | bytes 65568 | tf_op jit(solution)/shard_map/ppermute | solution.py:20
  29.3 1.1 %gram.1 = (f32[104,128]{1,0:T(8,128)S(1)}, f32[104,128]{1,0:T(8,128)S(1)}) custom-call(f32[128,128]{1,0:T(8,128)S(1)} %add_add_fusion.refs_0_, f32[128,128]{1,0:T(8,128)S(1)} %collective-permute-done.4.refs_1_, f32[128,128]{1,0:T(8,128)S(1)} %collective-permute-done.5.refs_2_, f32[128,128]{1,0:T(8,128)S(1)} %collective-permute-done.6.refs_3_, ...), custom_call_target="tpu_custom_call" | custom-call | tf_op jit(solution)/shard_map/gram/pallas_call | solution.py:208
  30.4 1.2 %collective-permute-done.10 = f32[104,128]{1,0:T(8,128)S(1)} collective-permute-done((f32[104,128]{1,0:T(8,128)S(1)}, f32[104,128]{1,0:T(8,128)S(1)}, u32[]{:S(2)}, u32[]{:S(2)}) %collective-permute-start.10) | collective-permute-done | bytes 53280 | tf_op jit(solution)/shard_map/ppermute | solution.py:20
  31.6 2.0 %collective-permute-start.13 = (f32[104,128]{1,0:T(8,128)S(1)}, f32[104,128]{1,0:T(8,128)S(1)}, u32[]{:S(2)}, u32[]{:S(2)}) collective-permute-start(f32[104,128]{1,0:T(8,128)S(1)} %add.56), channel_id=1, source_target_pairs={{0,3},{1,2},{2,1},{3,0},{4,7},{5,6},{6,5},{7,4},{8,11},{9,10},{10,... | collective-permute-start | bytes 159752 | tf_op jit(solution)/shard_map/ppermute | solution.py:20
  33.6 0.5 collective-permute-start.12
  34.1 2.0 %collective-permute-start.11 = (f32[104,128]{1,0:T(8,128)S(1)}, f32[104,128]{1,0:T(8,128)S(1)}, u32[]{:S(2)}, u32[]{:S(2)}) collective-permute-start(f32[104,128]{1,0:T(8,128)S(1)} %add.56), channel_id=1, source_target_pairs={{0,1},{1,0},{2,3},{3,2},{4,5},{5,4},{6,7},{7,6},{8,9},{9,8},{10,11... | collective-permute-start | bytes 159752 | tf_op jit(solution)/shard_map/ppermute | solution.py:20
  36.1 1.5 %collective-permute-start.17 = (bf16[32,4096]{1,0:T(8,128)(2,1)}, bf16[32,4096]{1,0:T(8,128)(2,1)S(1)}, u32[]{:S(2)}, u32[]{:S(2)}) collective-permute-start(bf16[32,4096]{1,0:T(8,128)(2,1)} %get-tuple-element.21), channel_id=1, source_target_pairs={{0,24},{8,16},{16,8},{24,0},{1,25},{9,17},{17,9},{25,1},{2,26},{10... | collective-permute-start | bytes 786440 | tf_op jit(solution)/shard_map/ppermute | solution.py:20
  37.6 0.5 collective-permute-start.16
  38.1 1.5 %collective-permute-start.15 = (bf16[32,4096]{1,0:T(8,128)(2,1)}, bf16[32,4096]{1,0:T(8,128)(2,1)S(1)}, u32[]{:S(2)}, u32[]{:S(2)}) collective-permute-start(bf16[32,4096]{1,0:T(8,128)(2,1)} %get-tuple-element.21), channel_id=1, source_target_pairs={{0,8},{8,0},{16,24},{24,16},{1,9},{9,1},{17,25},{25,17},{2,10},{10... | collective-permute-start | bytes 786440 | tf_op jit(solution)/shard_map/ppermute | solution.py:20
  39.8 6.6 %collective-permute-done.17.refs_5_ = bf16[32,4096]{1,0:T(8,128)(2,1)S(1)} collective-permute-done((bf16[32,4096]{1,0:T(8,128)(2,1)}, bf16[32,4096]{1,0:T(8,128)(2,1)S(1)}, u32[]{:S(2)}, u32[]{:S(2)}) %collective-permute-start.17) | collective-permute-done | bytes 262176 | tf_op jit(solution)/shard_map/ppermute | solution.py:20
  46.4 3.9 %collective-permute-done.16.refs_4_ = bf16[32,4096]{1,0:T(8,128)(2,1)S(1)} collective-permute-done((bf16[32,4096]{1,0:T(8,128)(2,1)}, bf16[32,4096]{1,0:T(8,128)(2,1)S(1)}, u32[]{:S(2)}, u32[]{:S(2)}) %collective-permute-start.16) | collective-permute-done | bytes 262176 | tf_op jit(solution)/shard_map/ppermute | solution.py:20
  50.4 6.0 %update.1 = (f32[32,4096]{1,0:T(8,128)}, f32[128,128]{1,0:T(8,128)}) custom-call(f32[104,128]{1,0:T(8,128)S(1)} %add_add_fusion.1.refs_0_, f32[104,128]{1,0:T(8,128)S(1)} %collective-permute-done.14.refs_1_, f32[32,4096]{1,0:T(8,128)S(1)} %copy-done, bf16[32,4096]{1,0:T(8,128)(2,1)S(1)} %collective-permute-done.15.refs_3_, ...), custom_call_target="tpu_custom_call" | custom-call | tf_op jit(solution)/shard_map/update/pallas_call | solution.py:309
  (27 shorter events, 2.2 us)
Async XLA Ops:
  0.6 49.8 %copy-start = (f32[32,4096]{1,0:T(8,128)S(1)}, f32[32,4096]{1,0:T(8,128)}, u32[]{:S(2)}) copy-start(f32[32,4096]{1,0:T(8,128)} %refs_2_.1) | copy-start | bytes 1572868
  0.6 15.2 %copy-start.1 = (f32[32,512]{1,0:T(8,128)S(1)}, f32[32,512]{1,0:T(8,128)}, u32[]{:S(2)}) copy-start(f32[32,512]{1,0:T(8,128)} %refs_4_) | copy-start | bytes 196612
  0.7 28.6 %copy-start.3 = (f32[512]{0:T(512)S(1)}, f32[512]{0:T(512)}, u32[]{:S(2)}) copy-start(f32[512]{0:T(512)} %param.12) | copy-start | bytes 6148
  0.7 28.6 %copy-start.2 = (f32[512]{0:T(512)S(1)}, f32[512]{0:T(512)}, u32[]{:S(2)}) copy-start(f32[512]{0:T(512)} %param.11) | copy-start | bytes 6148
  7.4 1.8 %collective-permute-start = (f32[4,128,128]{2,1,0:T(8,128)}, f32[4,128,128]{2,1,0:T(8,128)S(1)}, u32[]{:S(2)}, u32[]{:S(2)}) collective-permute-start(f32[4,128,128]{2,1,0:T(8,128)} %get-tuple-element.13), channel_id=1, source_target_pairs={{0,4},{4,0},{1,5},{5,1},{2,6},{6,2},{3,7},{7,3},{8,12},{12,8},{9,1... | collective-permute-start | bytes 786440 | tf_op jit(solution)/shard_map/ppermute | solution.py:20
  10.2 8.9 %collective-permute-start.1 = (f32[128,128]{1,0:T(8,128)S(1)}, f32[128,128]{1,0:T(8,128)S(1)}, u32[]{:S(2)}, u32[]{:S(2)}) collective-permute-start(f32[128,128]{1,0:T(8,128)S(1)} %get-tuple-element.15), channel_id=1, source_target_pairs={{0,1},{1,0},{2,3},{3,2},{4,5},{5,4},{6,7},{7,6},{8,9},{9,8},{10,11... | collective-permute-start | bytes 196616 | tf_op jit(solution)/shard_map/ppermute | solution.py:20
  13.4 7.5 %collective-permute-start.2 = (f32[128,128]{1,0:T(8,128)S(1)}, f32[128,128]{1,0:T(8,128)S(1)}, u32[]{:S(2)}, u32[]{:S(2)}) collective-permute-start(f32[128,128]{1,0:T(8,128)S(1)} %get-tuple-element.16), channel_id=1, source_target_pairs={{0,2},{1,3},{2,0},{3,1},{4,6},{5,7},{6,4},{7,5},{8,10},{9,11},{10,... | collective-permute-start | bytes 196616 | tf_op jit(solution)/shard_map/ppermute | solution.py:20
  15.8 6.2 %collective-permute-start.3 = (f32[128,128]{1,0:T(8,128)S(1)}, f32[128,128]{1,0:T(8,128)S(1)}, u32[]{:S(2)}, u32[]{:S(2)}) collective-permute-start(f32[128,128]{1,0:T(8,128)S(1)} %get-tuple-element.17), channel_id=1, source_target_pairs={{0,3},{1,2},{2,1},{3,0},{4,7},{5,6},{6,5},{7,4},{8,11},{9,10},{10,... | collective-permute-start | bytes 196616 | tf_op jit(solution)/shard_map/ppermute | solution.py:20
  15.8 9.1 %collective-permute-start.9 = (f32[32,512]{1,0:T(8,128)S(1)}, f32[32,512]{1,0:T(8,128)S(1)}, u32[]{:S(2)}, u32[]{:S(2)}) collective-permute-start(f32[32,512]{1,0:T(8,128)S(1)} %copy-done.1), channel_id=1, source_target_pairs={{0,24},{8,16},{16,8},{24,0},{1,25},{9,17},{17,9},{25,1},{2,26},{10... | collective-permute-start | bytes 196616 | tf_op jit(solution)/shard_map/ppermute | solution.py:20
  18.6 7.0 %collective-permute-start.8 = (f32[32,512]{1,0:T(8,128)S(1)}, f32[32,512]{1,0:T(8,128)S(1)}, u32[]{:S(2)}, u32[]{:S(2)}) collective-permute-start(f32[32,512]{1,0:T(8,128)S(1)} %copy-done.1), channel_id=1, source_target_pairs={{0,16},{8,24},{16,0},{24,8},{1,17},{9,25},{17,1},{25,9},{2,18},{10... | collective-permute-start | bytes 196616 | tf_op jit(solution)/shard_map/ppermute | solution.py:20
  19.1 6.4 %collective-permute-start.7 = (f32[32,512]{1,0:T(8,128)S(1)}, f32[32,512]{1,0:T(8,128)S(1)}, u32[]{:S(2)}, u32[]{:S(2)}) collective-permute-start(f32[32,512]{1,0:T(8,128)S(1)} %copy-done.1), channel_id=1, source_target_pairs={{0,8},{8,0},{16,24},{24,16},{1,9},{9,1},{17,25},{25,17},{2,10},{10... | collective-permute-start | bytes 196616 | tf_op jit(solution)/shard_map/ppermute | solution.py:20
  22.0 5.8 %collective-permute-start.6 = (f32[128,128]{1,0:T(8,128)S(1)}, f32[128,128]{1,0:T(8,128)S(1)}, u32[]{:S(2)}, u32[]{:S(2)}) collective-permute-start(f32[128,128]{1,0:T(8,128)S(1)} %add_add_fusion.refs_0_), channel_id=1, source_target_pairs={{0,24},{8,16},{16,8},{24,0},{1,25},{9,17},{17,9},{25,1},{2,26},{10... | collective-permute-start | bytes 196616 | tf_op jit(solution)/shard_map/ppermute | solution.py:20
  24.5 4.3 %collective-permute-start.5 = (f32[128,128]{1,0:T(8,128)S(1)}, f32[128,128]{1,0:T(8,128)S(1)}, u32[]{:S(2)}, u32[]{:S(2)}) collective-permute-start(f32[128,128]{1,0:T(8,128)S(1)} %add_add_fusion.refs_0_), channel_id=1, source_target_pairs={{0,16},{8,24},{16,0},{24,8},{1,17},{9,25},{17,1},{25,9},{2,18},{10... | collective-permute-start | bytes 196616 | tf_op jit(solution)/shard_map/ppermute | solution.py:20
  25.0 4.3 %collective-permute-start.4 = (f32[128,128]{1,0:T(8,128)S(1)}, f32[128,128]{1,0:T(8,128)S(1)}, u32[]{:S(2)}, u32[]{:S(2)}) collective-permute-start(f32[128,128]{1,0:T(8,128)S(1)} %add_add_fusion.refs_0_), channel_id=1, source_target_pairs={{0,8},{8,0},{16,24},{24,16},{1,9},{9,1},{17,25},{25,17},{2,10},{10... | collective-permute-start | bytes 196616 | tf_op jit(solution)/shard_map/ppermute | solution.py:20
  30.3 1.3 %collective-permute-start.10 = (f32[104,128]{1,0:T(8,128)S(1)}, f32[104,128]{1,0:T(8,128)S(1)}, u32[]{:S(2)}, u32[]{:S(2)}) collective-permute-start(f32[104,128]{1,0:T(8,128)S(1)} %get-tuple-element.20), channel_id=1, source_target_pairs={{0,4},{4,0},{1,5},{5,1},{2,6},{6,2},{3,7},{7,3},{8,12},{12,8},{9,1... | collective-permute-start | bytes 159752 | tf_op jit(solution)/shard_map/ppermute | solution.py:20
  31.6 6.5 %collective-permute-start.13 = (f32[104,128]{1,0:T(8,128)S(1)}, f32[104,128]{1,0:T(8,128)S(1)}, u32[]{:S(2)}, u32[]{:S(2)}) collective-permute-start(f32[104,128]{1,0:T(8,128)S(1)} %add.56), channel_id=1, source_target_pairs={{0,3},{1,2},{2,1},{3,0},{4,7},{5,6},{6,5},{7,4},{8,11},{9,10},{10,... | collective-permute-start | bytes 159752 | tf_op jit(solution)/shard_map/ppermute | solution.py:20
  33.6 6.1 %collective-permute-start.12 = (f32[104,128]{1,0:T(8,128)S(1)}, f32[104,128]{1,0:T(8,128)S(1)}, u32[]{:S(2)}, u32[]{:S(2)}) collective-permute-start(f32[104,128]{1,0:T(8,128)S(1)} %add.56), channel_id=1, source_target_pairs={{0,2},{1,3},{2,0},{3,1},{4,6},{5,7},{6,4},{7,5},{8,10},{9,11},{10,... | collective-permute-start | bytes 159752 | tf_op jit(solution)/shard_map/ppermute | solution.py:20
  34.1 5.5 %collective-permute-start.11 = (f32[104,128]{1,0:T(8,128)S(1)}, f32[104,128]{1,0:T(8,128)S(1)}, u32[]{:S(2)}, u32[]{:S(2)}) collective-permute-start(f32[104,128]{1,0:T(8,128)S(1)} %add.56), channel_id=1, source_target_pairs={{0,1},{1,0},{2,3},{3,2},{4,5},{5,4},{6,7},{7,6},{8,9},{9,8},{10,11... | collective-permute-start | bytes 159752 | tf_op jit(solution)/shard_map/ppermute | solution.py:20
  36.1 10.3 %collective-permute-start.17 = (bf16[32,4096]{1,0:T(8,128)(2,1)}, bf16[32,4096]{1,0:T(8,128)(2,1)S(1)}, u32[]{:S(2)}, u32[]{:S(2)}) collective-permute-start(bf16[32,4096]{1,0:T(8,128)(2,1)} %get-tuple-element.21), channel_id=1, source_target_pairs={{0,24},{8,16},{16,8},{24,0},{1,25},{9,17},{17,9},{25,1},{2,26},{10... | collective-permute-start | bytes 786440 | tf_op jit(solution)/shard_map/ppermute | solution.py:20
  37.6 12.7 %collective-permute-start.16 = (bf16[32,4096]{1,0:T(8,128)(2,1)}, bf16[32,4096]{1,0:T(8,128)(2,1)S(1)}, u32[]{:S(2)}, u32[]{:S(2)}) collective-permute-start(bf16[32,4096]{1,0:T(8,128)(2,1)} %get-tuple-element.21), channel_id=1, source_target_pairs={{0,16},{8,24},{16,0},{24,8},{1,17},{9,25},{17,1},{25,9},{2,18},{10... | collective-permute-start | bytes 786440 | tf_op jit(solution)/shard_map/ppermute | solution.py:20
  38.1 12.3 %collective-permute-start.15 = (bf16[32,4096]{1,0:T(8,128)(2,1)}, bf16[32,4096]{1,0:T(8,128)(2,1)S(1)}, u32[]{:S(2)}, u32[]{:S(2)}) collective-permute-start(bf16[32,4096]{1,0:T(8,128)(2,1)} %get-tuple-element.21), channel_id=1, source_target_pairs={{0,8},{8,0},{16,24},{24,16},{1,9},{9,1},{17,25},{25,17},{2,10},{10... | collective-permute-start | bytes 786440 | tf_op jit(solution)/shard_map/ppermute | solution.py:20
  39.7 10.7 %collective-permute-start.14 = (f32[104,128]{1,0:T(8,128)S(1)}, f32[104,128]{1,0:T(8,128)S(1)}, u32[]{:S(2)}, u32[]{:S(2)}) collective-permute-start(f32[104,128]{1,0:T(8,128)S(1)} %add_add_fusion.1.refs_0_), channel_id=1, source_target_pairs={{0,4},{4,0},{1,5},{5,1},{2,6},{6,2},{3,7},{7,3},{8,12},{12,8},{9,1... | collective-permute-start | bytes 159752 | tf_op jit(solution)/shard_map/ppermute | solution.py:20

commit v3 on v2

--- a/solution.py
+++ b/solution.py
@@ -37,8 +37,8 @@
 def contribute_kernel(
     owned,
     depth,
-    pattern_ref,
-    ownership_ref,
+    slots,
+    table,
     prior_hbm,
     sens_hbm,
     keep_ref,
@@ -51,7 +51,7 @@
     sens_sems,
     prior_sems,
 ):
-    blocks, slots = pattern_ref.shape
+    blocks = sens.shape[0]
     tiles, _, lanes = keep_ref.shape
     members_dev = prior.shape[0]
     _, rows_block, params = sens.shape
@@ -74,10 +74,10 @@
             copy.start()
 
     def place(s, carry):
-        storage[ownership_ref[s]] = s ^ (me * owned)
+        storage[table[blocks, s]] = s ^ (me * owned)
         return carry
 
-    lax.fori_loop(0, ownership_ref.shape[0], place, 0, unroll=8)
+    lax.fori_loop(0, storage.shape[0], place, 0, unroll=8)
     acc[...] = jnp.zeros_like(acc)
     lane_group = lax.broadcasted_iota(jnp.int32, (obs_block, lanes), 1) // members_dev
 
@@ -98,7 +98,7 @@
                 sens[b, : count * obs_block], rows, NT, preferred_element_type=jnp.float32
             )
             for k in range(count):
-                block = pattern_ref[b, k]
+                block = table[b, k]
                 at = storage[jnp.maximum(block, 0)]
                 group = jnp.where(block >= 0, (at % owned) // groups, -1)
                 acc[(at // owned) * groups + at % groups] += jnp.where(
@@ -107,9 +107,9 @@
 
         counts = list(range(slots // 4, slots + 1, 4))
         for low, count in zip([0] + counts[:-1], counts):
-            fits = (low == 0) | (pattern_ref[b, low] >= 0)
+            fits = (low == 0) | (table[b, low] >= 0)
             if count < slots:
-                fits = fits & (pattern_ref[b, count] < 0)
+                fits = fits & (table[b, count] < 0)
             pl.when(fits)(functools.partial(add, count))
         return carry
 
@@ -125,20 +125,27 @@
     lax.fori_loop(0, tiles, flush, 0, unroll=4)
 
 
-def contribute(prior, sensitivity, pattern, ownership, obs_dev):
+def contribute(prior, sensitivity, pattern, ownership, perturbation):
     members_dev = prior.shape[0]
     blocks, slots, obs_block, params = sensitivity.shape
     tiles = lax.axis_size("tile")
+    obs_dev = perturbation.shape[1]
     owned = obs_dev // obs_block
     lanes = 128
     groups = owned // (lanes // members_dev)
     half = jax.ShapeDtypeStruct((tiles, groups * obs_block, lanes), jnp.float32)
+    total = ownership.shape[0]
+    table = jnp.concatenate([jnp.pad(pattern, ((0, 0), (0, total - slots))), ownership[None]])
     hbm = pl.BlockSpec(memory_space=pl.ANY)
     return pl.pallas_call(
-        functools.partial(contribute_kernel, owned, min(3, blocks)),
-        in_specs=[SMEM, SMEM, hbm, hbm],
+        functools.partial(contribute_kernel, owned, min(3, blocks), slots),
+        in_specs=[SMEM, hbm, hbm],
         out_specs=[VMEM, VMEM, VMEM],
-        out_shape=[half, half, jax.ShapeDtypeStruct(prior.shape, jnp.bfloat16)],
+        out_shape=[
+            half,
+            half,
+            jax.ShapeDtypeStruct((members_dev, prior.shape[1] + obs_dev), jnp.bfloat16),
+        ],
         scratch_shapes=[
             pltpu.VMEM((blocks, slots * obs_block, params), jnp.bfloat16),
             pltpu.VMEM(prior.shape, jnp.float32),
@@ -147,8 +154,9 @@
             pltpu.SemaphoreType.DMA((blocks,)),
             pltpu.SemaphoreType.DMA((blocks,)),
         ],
+        compiler_params=pltpu.CompilerParams(vmem_limit_bytes=54272 << 10),
         name="contribute",
-    )(pattern, ownership, prior, sensitivity.reshape(blocks, slots * obs_block, params))
+    )(table, prior, sensitivity.reshape(blocks, slots * obs_block, params))
 
 
 def gram_kernel(count, *refs):
@@ -166,7 +174,7 @@
                 q * members_dev : (q + 1) * members_dev
             ]
         whole_rows = pl.ds(pl.multiple_of(members + (at ^ r) * members_dev, members_dev), members_dev)
-        stack[whole_rows, :] = noise[r][...]
+        stack[whole_rows, :] = noise[r][:, -stack.shape[1] :].astype(jnp.float32)
     values = stack[:members, :]
     inverse = 1.0 / sigma[...]
     spread = (values - jnp.mean(values, axis=0, keepdims=True)) * (
@@ -202,7 +210,7 @@
 
 def gram(predicted, noise, observed, sigma):
     count = len(predicted)
-    members_dev, obs_dev = noise[0].shape
+    members_dev, obs_dev = noise[0].shape[0], observed.shape[0]
     members = members_dev * count
     half = jax.ShapeDtypeStruct((members // 2 + members // 4 + 8, members), jnp.float32)
     return pl.pallas_call(
@@ -230,7 +238,7 @@
     own_rows = pl.ds(pl.multiple_of(at * members_dev, members_dev), members_dev)
     for r in range(count):
         rows = pl.ds(pl.multiple_of((at ^ r) * members_dev, members_dev), members_dev)
-        ensemble[rows, :] = prior[r][...].astype(jnp.bfloat16)
+        ensemble[rows, :] = prior[r][:, : ensemble.shape[1]]
     half, quarter = members // 2, members // 4
     for part, at_side in ((mine, side), (other, 1 - side)):
         cross[pl.ds(pl.multiple_of(at_side * half, half), half), :] = part[:half, :]
@@ -302,9 +310,9 @@
         increment[:, lanes] = jnp.dot(own, ensemble[:, lanes], preferred_element_type=jnp.float32)
 
 
-def update(mine, other, prior):
+def update(mine, other, prior, params):
     count = len(prior)
-    members_dev, params = prior[0].shape
+    members_dev = prior[0].shape[0]
     members = members_dev * count
     return pl.pallas_call(
         functools.partial(update_kernel, count),
@@ -328,14 +336,12 @@
 
 
 def step(prior, sensitivity, pattern, ownership, observed, obs_noise, perturbation):
-    obs_dev = observed.shape[0]
     tiles = lax.axis_size("tile")
-    keep, send, prior_bf = contribute(prior, sensitivity, pattern, ownership, obs_dev)
+    keep, send, own = contribute(prior, sensitivity, pattern, ownership, perturbation)
+    own = lax.dynamic_update_slice(own, perturbation.astype(own.dtype), (0, prior.shape[1]))
     got = swap(send, "slab", 1)
     chunks = [keep[r] + got[r] for r in range(tiles)]
-    chunks, perturbation = lax.optimization_barrier((chunks, perturbation))
-    noise = gather_xor(perturbation, "member")
-    ensemble = [prior] + gather_xor(prior_bf, "member")[1:]
+    ensemble = gather_xor(own, "member")
     for shift, radix in digits(tiles):
         low = 1 << shift
         arrived = [
@@ -344,11 +350,11 @@
         ]
         chunks = [sum((g[r] for g in arrived), chunks[r]) for r in range(low)]
     predicted = gather_xor(chunks[0], "member")
-    keep, send = gram(predicted, noise, observed, obs_noise)
+    keep, send = gram(predicted, ensemble, observed, obs_noise)
     mine = keep + swap(send, "slab", 1)
     for shift, radix in digits(tiles)[::-1]:
         mine = sum((swap(mine, "tile", d << shift) for d in range(1, radix)), mine)
-    return tuple(update(mine, swap(mine, "slab", 1), ensemble))
+    return tuple(update(mine, swap(mine, "slab", 1), ensemble, prior.shape[1]))
 
 
 def solution(mesh):

time: 56.6 us -> 51.4 us (0.908)
  starting transfers between devices: 21.2 us -> 18.6 us
  waiting for transfers between devices: 19.6 us -> 18.3 us
  Pallas kernels: 13.8 us -> 12.7 us
    ppermute x18 -> x15, starting transfers between devices: 21.2 us -> 18.6 us  [swap(): return lax.ppermute(x, axis, [(i, i ^ distance) for i in range(size)])]
    ppermute x18 -> x15, waiting for transfers between devices: 19.6 us -> 18.3 us  [swap(): return lax.ppermute(x, axis, [(i, i ^ distance) for i in range(size)])]
    pallas_call x1, Pallas kernels: 6.76 us -> 5.69 us  [contribute(): pl.pallas_call(functools.partial(contribute_kernel, owned, min(3, blocks)...]
    add x1, other arithmetic: 0.98 us -> 0.03 us  [step(): chunks = [keep[r] + got[r] for r in range(tiles)]]
    concatenate x0 -> x1, other arithmetic: none -> 0.73 us  [contribute(): jnp.concatenate([jnp.pad(pattern, ((0, 0), (0, total - slots))), ownershi...]
  transfers between devices with their start and end apart: 18 -> 15, of which waited for: 11 -> 13; matrix products, arithmetic and copies ran while one was open for 0% -> 0% of each run, Pallas kernels for 0% -> 0%
where the time goes in v3:
time: 51.4 us; the launch traced here: 51.2 us
  starting transfers between devices  18.6 us (36%)
  waiting for transfers between devices  18.3 us (36%)
  Pallas kernels  12.7 us (25%)
  other arithmetic  0.81 us (2%)
  between operations  0.71 us (1%)
    ppermute x15, starting transfers between devices, swap(): return lax.ppermute(x, axis, [(i, i ^ distance) for i in range(size)])  18.6 us
    ppermute x15, waiting for transfers between devices, swap(): return lax.ppermute(x, axis, [(i, i ^ distance) for i in range(size)])  18.3 us
    pallas_call x1, Pallas kernels, update(): pl.pallas_call(functools.partial(update_kernel, count), in_specs=[VMEM] *...  5.97 us
    pallas_call x1, Pallas kernels, contribute(): pl.pallas_call(functools.partial(contribute_kernel, owned, min(3, blocks)...  5.69 us
    pallas_call x1, Pallas kernels, gram(): pl.pallas_call(functools.partial(gram_kernel, count), in_specs=[VMEM] * (...  1.06 us
  transfers between devices with their start and end apart: 15, of which 13 were waited for; matrix products, arithmetic and copies ran while one was open for 0% of the time, Pallas kernels for 0%

profile of v3, /device:TPU:0, one launch (start us, length us, event | category | flops | bytes accessed | tf_op | source)
XLA Modules:
  0.0 51.2 jit_solution(3185204552398676487)
XLA Ops:
  0.7 0.7 %pad_add_fusion.table = s32[9,64]{1,0:T(8,128)S(1)} fusion(s32[8,16]{1,0:T(8,128)} %param.9, s32[1,64]{1,0:T(1,128)} %bitcast.21), kind=kLoop, calls=%fused_computation.13 | loop fusion | flops 576 | bytes 3072 | tf_op jit(solution)/shard_map/concatenate | solution.py:138
  1.4 5.7 %contribute.1 = (f32[4,128,128]{2,1,0:T(8,128)S(1)}, f32[4,128,128]{2,1,0:T(8,128)S(1)}, bf16[32,4608]{1,0:T(8,128)(2,1)S(1)}) custom-call(s32[9,64]{1,0:T(8,128)S(1)} %pad_add_fusion.table, f32[32,4096]{1,0:T(8,128)} %prior_hbm.1, bf16[8,1024,512]{2,1,0:T(8,128)(2,1)} %bitcast.20), custom_call_target="tpu_custom_call" | custom-call | tf_op jit(solution)/shard_map/contribute/pallas_call | solution.py:140
  7.5 1.2 %collective-permute-done = f32[4,128,128]{2,1,0:T(8,128)S(1)} collective-permute-done((f32[4,128,128]{2,1,0:T(8,128)S(1)}, f32[4,128,128]{2,1,0:T(8,128)S(1)}, u32[]{:S(2)}, u32[]{:S(2)}) %collective-permute-start) | collective-permute-done | bytes 262176 | tf_op jit(solution)/shard_map/ppermute | solution.py:20
  8.7 3.2 %collective-permute-start.1 = (f32[128,128]{1,0:T(8,128)S(1)}, f32[128,128]{1,0:T(8,128)S(1)}, u32[]{:S(2)}, u32[]{:S(2)}) collective-permute-start(f32[128,128]{1,0:T(8,128)S(1)} %get-tuple-element.12), channel_id=1, source_target_pairs={{0,1},{1,0},{2,3},{3,2},{4,5},{5,4},{6,7},{7,6},{8,9},{9,8},{10,11... | collective-permute-start | bytes 196616 | tf_op jit(solution)/shard_map/ppermute | solution.py:20
  11.9 2.2 %collective-permute-start.3 = (f32[128,128]{1,0:T(8,128)S(1)}, f32[128,128]{1,0:T(8,128)S(1)}, u32[]{:S(2)}, u32[]{:S(2)}) collective-permute-start(f32[128,128]{1,0:T(8,128)S(1)} %get-tuple-element.13), channel_id=1, source_target_pairs={{0,3},{1,2},{2,1},{3,0},{4,7},{5,6},{6,5},{7,4},{8,11},{9,10},{10,... | collective-permute-start | bytes 196616 | tf_op jit(solution)/shard_map/ppermute | solution.py:20
  14.3 2.5 %collective-permute-start.9 = (bf16[32,4608]{1,0:T(8,128)(2,1)S(1)}, bf16[32,4608]{1,0:T(8,128)(2,1)S(1)}, u32[]{:S(2)}, u32[]{:S(2)}) collective-permute-start(bf16[32,4608]{1,0:T(8,128)(2,1)S(1)} %convert_dynamic-update-slice_fusion.refs_4_.refs_2_), channel_id=1, source_target_pairs={{0,24},{8,16},{16,8},{24,0},{1,25},{9,17},{17,9},{25,1},{2,26},{10... | collective-permute-start | bytes 884744 | tf_op jit(solution)/shard_map/ppermute | solution.py:20
  17.3 0.6 %collective-permute-start.7 = (bf16[32,4608]{1,0:T(8,128)(2,1)S(1)}, bf16[32,4608]{1,0:T(8,128)(2,1)S(1)}, u32[]{:S(2)}, u32[]{:S(2)}) collective-permute-start(bf16[32,4608]{1,0:T(8,128)(2,1)S(1)} %convert_dynamic-update-slice_fusion.refs_4_.refs_2_), channel_id=1, source_target_pairs={{0,8},{8,0},{16,24},{24,16},{1,9},{9,1},{17,25},{25,17},{2,10},{10... | collective-permute-start | bytes 884744 | tf_op jit(solution)/shard_map/ppermute | solution.py:20
  17.9 0.7 %collective-permute-done.3 = f32[128,128]{1,0:T(8,128)S(1)} collective-permute-done((f32[128,128]{1,0:T(8,128)S(1)}, f32[128,128]{1,0:T(8,128)S(1)}, u32[]{:S(2)}, u32[]{:S(2)}) %collective-permute-start.3) | collective-permute-done | bytes 65568 | tf_op jit(solution)/shard_map/ppermute | solution.py:20
  18.5 2.2 %collective-permute-done.2 = f32[128,128]{1,0:T(8,128)S(1)} collective-permute-done((f32[128,128]{1,0:T(8,128)S(1)}, f32[128,128]{1,0:T(8,128)S(1)}, u32[]{:S(2)}, u32[]{:S(2)}) %collective-permute-start.2) | collective-permute-done | bytes 65568 | tf_op jit(solution)/shard_map/ppermute | solution.py:20
  20.8 2.5 %collective-permute-start.6 = (f32[128,128]{1,0:T(8,128)S(1)}, f32[128,128]{1,0:T(8,128)S(1)}, u32[]{:S(2)}, u32[]{:S(2)}) collective-permute-start(f32[128,128]{1,0:T(8,128)S(1)} %fusion.6.refs_0_), channel_id=1, source_target_pairs={{0,24},{8,16},{16,8},{24,0},{1,25},{9,17},{17,9},{25,1},{2,26},{10... | collective-permute-start | bytes 196616 | tf_op jit(solution)/shard_map/ppermute | solution.py:20
  23.8 1.4 %collective-permute-done.9.refs_7_.refs_5_ = bf16[32,4608]{1,0:T(8,128)(2,1)S(1)} collective-permute-done((bf16[32,4608]{1,0:T(8,128)(2,1)S(1)}, bf16[32,4608]{1,0:T(8,128)(2,1)S(1)}, u32[]{:S(2)}, u32[]{:S(2)}) %collective-permute-start.9) | collective-permute-done | bytes 294944 | tf_op jit(solution)/shard_map/ppermute | solution.py:20
  25.2 1.5 %collective-permute-start.4 = (f32[128,128]{1,0:T(8,128)S(1)}, f32[128,128]{1,0:T(8,128)S(1)}, u32[]{:S(2)}, u32[]{:S(2)}) collective-permute-start(f32[128,128]{1,0:T(8,128)S(1)} %fusion.6.refs_0_), channel_id=1, source_target_pairs={{0,8},{8,0},{16,24},{24,16},{1,9},{9,1},{17,25},{25,17},{2,10},{10... | collective-permute-start | bytes 196616 | tf_op jit(solution)/shard_map/ppermute | solution.py:20
  26.7 4.2 %collective-permute-done.8.refs_6_.refs_4_ = bf16[32,4608]{1,0:T(8,128)(2,1)S(1)} collective-permute-done((bf16[32,4608]{1,0:T(8,128)(2,1)S(1)}, bf16[32,4608]{1,0:T(8,128)(2,1)S(1)}, u32[]{:S(2)}, u32[]{:S(2)}) %collective-permute-start.8) | collective-permute-done | bytes 294944 | tf_op jit(solution)/shard_map/ppermute | solution.py:20
  30.9 0.7 %collective-permute-done.7.refs_5_.refs_3_ = bf16[32,4608]{1,0:T(8,128)(2,1)S(1)} collective-permute-done((bf16[32,4608]{1,0:T(8,128)(2,1)S(1)}, bf16[32,4608]{1,0:T(8,128)(2,1)S(1)}, u32[]{:S(2)}, u32[]{:S(2)}) %collective-permute-start.7) | collective-permute-done | bytes 294944 | tf_op jit(solution)/shard_map/ppermute | solution.py:20
  31.5 0.8 %collective-permute-done.6.refs_3_ = f32[128,128]{1,0:T(8,128)S(1)} collective-permute-done((f32[128,128]{1,0:T(8,128)S(1)}, f32[128,128]{1,0:T(8,128)S(1)}, u32[]{:S(2)}, u32[]{:S(2)}) %collective-permute-start.6) | collective-permute-done | bytes 65568 | tf_op jit(solution)/shard_map/ppermute | solution.py:20
  32.3 0.6 %collective-permute-done.5.refs_2_ = f32[128,128]{1,0:T(8,128)S(1)} collective-permute-done((f32[128,128]{1,0:T(8,128)S(1)}, f32[128,128]{1,0:T(8,128)S(1)}, u32[]{:S(2)}, u32[]{:S(2)}) %collective-permute-start.5) | collective-permute-done | bytes 65568 | tf_op jit(solution)/shard_map/ppermute | solution.py:20
  33.0 1.1 %gram.1 = (f32[104,128]{1,0:T(8,128)S(1)}, f32[104,128]{1,0:T(8,128)S(1)}) custom-call(f32[128,128]{1,0:T(8,128)S(1)} %fusion.6.refs_0_, f32[128,128]{1,0:T(8,128)S(1)} %collective-permute-done.4.refs_1_, f32[128,128]{1,0:T(8,128)S(1)} %collective-permute-done.5.refs_2_, f32[128,128]{1,0:T(8,128)S(1)} %collective-permute-done.6.refs_3_, ...), custom_call_target="tpu_custom_call" | custom-call | tf_op jit(solution)/shard_map/gram/pallas_call | solution.py:216
  34.1 1.2 %collective-permute-done.10 = f32[104,128]{1,0:T(8,128)S(1)} collective-permute-done((f32[104,128]{1,0:T(8,128)S(1)}, f32[104,128]{1,0:T(8,128)S(1)}, u32[]{:S(2)}, u32[]{:S(2)}) %collective-permute-start.10) | collective-permute-done | bytes 53280 | tf_op jit(solution)/shard_map/ppermute | solution.py:20
  35.3 2.7 %collective-permute-start.13 = (f32[104,128]{1,0:T(8,128)S(1)}, f32[104,128]{1,0:T(8,128)S(1)}, u32[]{:S(2)}, u32[]{:S(2)}) collective-permute-start(f32[104,128]{1,0:T(8,128)S(1)} %add.58), channel_id=1, source_target_pairs={{0,3},{1,2},{2,1},{3,0},{4,7},{5,6},{6,5},{7,4},{8,11},{9,10},{10,... | collective-permute-start | bytes 159752 | tf_op jit(solution)/shard_map/ppermute | solution.py:20
  38.6 1.2 %collective-permute-start.11 = (f32[104,128]{1,0:T(8,128)S(1)}, f32[104,128]{1,0:T(8,128)S(1)}, u32[]{:S(2)}, u32[]{:S(2)}) collective-permute-start(f32[104,128]{1,0:T(8,128)S(1)} %add.58), channel_id=1, source_target_pairs={{0,1},{1,0},{2,3},{3,2},{4,5},{5,4},{6,7},{7,6},{8,9},{9,8},{10,11... | collective-permute-start | bytes 159752 | tf_op jit(solution)/shard_map/ppermute | solution.py:20
  39.8 1.7 %collective-permute-done.13 = f32[104,128]{1,0:T(8,128)S(1)} collective-permute-done((f32[104,128]{1,0:T(8,128)S(1)}, f32[104,128]{1,0:T(8,128)S(1)}, u32[]{:S(2)}, u32[]{:S(2)}) %collective-permute-start.13) | collective-permute-done | bytes 53280 | tf_op jit(solution)/shard_map/ppermute | solution.py:20
  41.5 2.4 %collective-permute-done.12 = f32[104,128]{1,0:T(8,128)S(1)} collective-permute-done((f32[104,128]{1,0:T(8,128)S(1)}, f32[104,128]{1,0:T(8,128)S(1)}, u32[]{:S(2)}, u32[]{:S(2)}) %collective-permute-start.12) | collective-permute-done | bytes 53280 | tf_op jit(solution)/shard_map/ppermute | solution.py:20
  44.0 1.2 %collective-permute-done.14.refs_1_ = f32[104,128]{1,0:T(8,128)S(1)} collective-permute-done((f32[104,128]{1,0:T(8,128)S(1)}, f32[104,128]{1,0:T(8,128)S(1)}, u32[]{:S(2)}, u32[]{:S(2)}) %collective-permute-start.14) | collective-permute-done | bytes 53280 | tf_op jit(solution)/shard_map/ppermute | solution.py:20
  45.2 6.0 %update.1 = (f32[32,4096]{1,0:T(8,128)}, f32[128,128]{1,0:T(8,128)}) custom-call(f32[104,128]{1,0:T(8,128)S(1)} %add_add_fusion.refs_0_, f32[104,128]{1,0:T(8,128)S(1)} %collective-permute-done.14.refs_1_, bf16[32,4608]{1,0:T(8,128)(2,1)S(1)} %convert_dynamic-update-slice_fusion.refs_4_.refs_2_, bf16[32,4608]{1,0:T(8,128)(2,1)S(1)} %collective-permute-done.7.refs_5_.refs_3_, ...), custom_call_target="tpu_custom_call" | custom-call | tf_op jit(solution)/shard_map/update/pallas_call | solution.py:317
  (21 shorter events, 2.5 us)
Async XLA Ops:
  0.6 13.7 %copy-start.2 = (f32[32,512]{1,0:T(8,128)S(1)}, f32[32,512]{1,0:T(8,128)}, u32[]{:S(2)}) copy-start(f32[32,512]{1,0:T(8,128)} %param.13) | copy-start | bytes 196612
  0.6 32.3 %copy-start.1 = (f32[512]{0:T(512)S(1)}, f32[512]{0:T(512)}, u32[]{:S(2)}) copy-start(f32[512]{0:T(512)} %param.12) | copy-start | bytes 6148
  0.7 32.3 %copy-start = (f32[512]{0:T(512)S(1)}, f32[512]{0:T(512)}, u32[]{:S(2)}) copy-start(f32[512]{0:T(512)} %param.11) | copy-start | bytes 6148
  7.1 1.6 %collective-permute-start = (f32[4,128,128]{2,1,0:T(8,128)S(1)}, f32[4,128,128]{2,1,0:T(8,128)S(1)}, u32[]{:S(2)}, u32[]{:S(2)}) collective-permute-start(f32[4,128,128]{2,1,0:T(8,128)S(1)} %get-tuple-element.8), channel_id=1, source_target_pairs={{0,4},{4,0},{1,5},{5,1},{2,6},{6,2},{3,7},{7,3},{8,12},{12,8},{9,1... | collective-permute-start | bytes 786440 | tf_op jit(solution)/shard_map/ppermute | solution.py:20
  8.7 8.6 %collective-permute-start.1 = (f32[128,128]{1,0:T(8,128)S(1)}, f32[128,128]{1,0:T(8,128)S(1)}, u32[]{:S(2)}, u32[]{:S(2)}) collective-permute-start(f32[128,128]{1,0:T(8,128)S(1)} %get-tuple-element.12), channel_id=1, source_target_pairs={{0,1},{1,0},{2,3},{3,2},{4,5},{5,4},{6,7},{7,6},{8,9},{9,8},{10,11... | collective-permute-start | bytes 196616 | tf_op jit(solution)/shard_map/ppermute | solution.py:20
  11.9 6.6 %collective-permute-start.3 = (f32[128,128]{1,0:T(8,128)S(1)}, f32[128,128]{1,0:T(8,128)S(1)}, u32[]{:S(2)}, u32[]{:S(2)}) collective-permute-start(f32[128,128]{1,0:T(8,128)S(1)} %get-tuple-element.13), channel_id=1, source_target_pairs={{0,3},{1,2},{2,1},{3,0},{4,7},{5,6},{6,5},{7,4},{8,11},{9,10},{10,... | collective-permute-start | bytes 196616 | tf_op jit(solution)/shard_map/ppermute | solution.py:20
  14.0 6.7 %collective-permute-start.2 = (f32[128,128]{1,0:T(8,128)S(1)}, f32[128,128]{1,0:T(8,128)S(1)}, u32[]{:S(2)}, u32[]{:S(2)}) collective-permute-start(f32[128,128]{1,0:T(8,128)S(1)} %get-tuple-element.14), channel_id=1, source_target_pairs={{0,2},{1,3},{2,0},{3,1},{4,6},{5,7},{6,4},{7,5},{8,10},{9,11},{10,... | collective-permute-start | bytes 196616 | tf_op jit(solution)/shard_map/ppermute | solution.py:20
  14.3 10.9 %collective-permute-start.9 = (bf16[32,4608]{1,0:T(8,128)(2,1)S(1)}, bf16[32,4608]{1,0:T(8,128)(2,1)S(1)}, u32[]{:S(2)}, u32[]{:S(2)}) collective-permute-start(bf16[32,4608]{1,0:T(8,128)(2,1)S(1)} %convert_dynamic-update-slice_fusion.refs_4_.refs_2_), channel_id=1, source_target_pairs={{0,24},{8,16},{16,8},{24,0},{1,25},{9,17},{17,9},{25,1},{2,26},{10... | collective-permute-start | bytes 884744 | tf_op jit(solution)/shard_map/ppermute | solution.py:20
  16.8 14.1 %collective-permute-start.8 = (bf16[32,4608]{1,0:T(8,128)(2,1)S(1)}, bf16[32,4608]{1,0:T(8,128)(2,1)S(1)}, u32[]{:S(2)}, u32[]{:S(2)}) collective-permute-start(bf16[32,4608]{1,0:T(8,128)(2,1)S(1)} %convert_dynamic-update-slice_fusion.refs_4_.refs_2_), channel_id=1, source_target_pairs={{0,16},{8,24},{16,0},{24,8},{1,17},{9,25},{17,1},{25,9},{2,18},{10... | collective-permute-start | bytes 884744 | tf_op jit(solution)/shard_map/ppermute | solution.py:20
  17.3 14.2 %collective-permute-start.7 = (bf16[32,4608]{1,0:T(8,128)(2,1)S(1)}, bf16[32,4608]{1,0:T(8,128)(2,1)S(1)}, u32[]{:S(2)}, u32[]{:S(2)}) collective-permute-start(bf16[32,4608]{1,0:T(8,128)(2,1)S(1)} %convert_dynamic-update-slice_fusion.refs_4_.refs_2_), channel_id=1, source_target_pairs={{0,8},{8,0},{16,24},{24,16},{1,9},{9,1},{17,25},{25,17},{2,10},{10... | collective-permute-start | bytes 884744 | tf_op jit(solution)/shard_map/ppermute | solution.py:20
  20.8 11.6 %collective-permute-start.6 = (f32[128,128]{1,0:T(8,128)S(1)}, f32[128,128]{1,0:T(8,128)S(1)}, u32[]{:S(2)}, u32[]{:S(2)}) collective-permute-start(f32[128,128]{1,0:T(8,128)S(1)} %fusion.6.refs_0_), channel_id=1, source_target_pairs={{0,24},{8,16},{16,8},{24,0},{1,25},{9,17},{17,9},{25,1},{2,26},{10... | collective-permute-start | bytes 196616 | tf_op jit(solution)/shard_map/ppermute | solution.py:20
  23.3 9.6 %collective-permute-start.5 = (f32[128,128]{1,0:T(8,128)S(1)}, f32[128,128]{1,0:T(8,128)S(1)}, u32[]{:S(2)}, u32[]{:S(2)}) collective-permute-start(f32[128,128]{1,0:T(8,128)S(1)} %fusion.6.refs_0_), channel_id=1, source_target_pairs={{0,16},{8,24},{16,0},{24,8},{1,17},{9,25},{17,1},{25,9},{2,18},{10... | collective-permute-start | bytes 196616 | tf_op jit(solution)/shard_map/ppermute | solution.py:20
  25.2 7.8 %collective-permute-start.4 = (f32[128,128]{1,0:T(8,128)S(1)}, f32[128,128]{1,0:T(8,128)S(1)}, u32[]{:S(2)}, u32[]{:S(2)}) collective-permute-start(f32[128,128]{1,0:T(8,128)S(1)} %fusion.6.refs_0_), channel_id=1, source_target_pairs={{0,8},{8,0},{16,24},{24,16},{1,9},{9,1},{17,25},{25,17},{2,10},{10... | collective-permute-start | bytes 196616 | tf_op jit(solution)/shard_map/ppermute | solution.py:20
  34.0 1.3 %collective-permute-start.10 = (f32[104,128]{1,0:T(8,128)S(1)}, f32[104,128]{1,0:T(8,128)S(1)}, u32[]{:S(2)}, u32[]{:S(2)}) collective-permute-start(f32[104,128]{1,0:T(8,128)S(1)} %get-tuple-element.11), channel_id=1, source_target_pairs={{0,4},{4,0},{1,5},{5,1},{2,6},{6,2},{3,7},{7,3},{8,12},{12,8},{9,1... | collective-permute-start | bytes 159752 | tf_op jit(solution)/shard_map/ppermute | solution.py:20
  35.3 6.2 %collective-permute-start.13 = (f32[104,128]{1,0:T(8,128)S(1)}, f32[104,128]{1,0:T(8,128)S(1)}, u32[]{:S(2)}, u32[]{:S(2)}) collective-permute-start(f32[104,128]{1,0:T(8,128)S(1)} %add.58), channel_id=1, source_target_pairs={{0,3},{1,2},{2,1},{3,0},{4,7},{5,6},{6,5},{7,4},{8,11},{9,10},{10,... | collective-permute-start | bytes 159752 | tf_op jit(solution)/shard_map/ppermute | solution.py:20
  38.1 5.9 %collective-permute-start.12 = (f32[104,128]{1,0:T(8,128)S(1)}, f32[104,128]{1,0:T(8,128)S(1)}, u32[]{:S(2)}, u32[]{:S(2)}) collective-permute-start(f32[104,128]{1,0:T(8,128)S(1)} %add.58), channel_id=1, source_target_pairs={{0,2},{1,3},{2,0},{3,1},{4,6},{5,7},{6,4},{7,5},{8,10},{9,11},{10,... | collective-permute-start | bytes 159752 | tf_op jit(solution)/shard_map/ppermute | solution.py:20
  38.6 5.3 %collective-permute-start.11 = (f32[104,128]{1,0:T(8,128)S(1)}, f32[104,128]{1,0:T(8,128)S(1)}, u32[]{:S(2)}, u32[]{:S(2)}) collective-permute-start(f32[104,128]{1,0:T(8,128)S(1)} %add.58), channel_id=1, source_target_pairs={{0,1},{1,0},{2,3},{3,2},{4,5},{5,4},{6,7},{7,6},{8,9},{9,8},{10,11... | collective-permute-start | bytes 159752 | tf_op jit(solution)/shard_map/ppermute | solution.py:20
  43.9 1.3 %collective-permute-start.14 = (f32[104,128]{1,0:T(8,128)S(1)}, f32[104,128]{1,0:T(8,128)S(1)}, u32[]{:S(2)}, u32[]{:S(2)}) collective-permute-start(f32[104,128]{1,0:T(8,128)S(1)} %add_add_fusion.refs_0_), channel_id=1, source_target_pairs={{0,4},{4,0},{1,5},{5,1},{2,6},{6,2},{3,7},{7,3},{8,12},{12,8},{9,1... | collective-permute-start | bytes 159752 | tf_op jit(solution)/shard_map/ppermute | solution.py:20
